TPU v7x, 128 devices: a whole 4x4x4 slice. The times are simulated.
128 devices in a mesh: tx: 8 (over y, core), ty: 16 (over z, x).
Axes of the slice: x: 4, y: 4, z: 4, core: 2. Of those that a mesh axis runs over, the one named last changes fastest.
Arguments:
- increments: bfloat16 [3, 8, 1152, 4096], P(None, None, 'tx', 'ty'), may hold values from -6 to 6
- remap_weights: bfloat16 [8, 16, 144, 2, 128, 256], P('tx', 'ty'), may hold values from -0.375 to 0.375
- dest_offset: int32 [8, 16, 144, 2], P('tx', 'ty'), may hold values from 0 to 3, as said below
- slot_patch: int32 [8, 16, 4, 108], P('tx', 'ty'), may hold values from 0 to 143, as said below
- rotation: int32 [2, 4], replicated, may hold values from 0 to 3
- basis: float32 [4, 768, 3072], P(None, 'ty', 'tx'), may hold values from -4 to 4
- inv_metric_diag: float32 [2, 768, 3072], P(None, 'ty', 'tx'), may hold values from 0.7 to 1.7
- inv_metric_cross: float32 [768, 3072], P('ty', 'tx'), may hold values from -0.5 to 0.5
- thickness: float32 [8, 768, 3072], P(None, 'ty', 'tx'), may hold values from -6 to 6
- wind_first: float32 [8, 768, 3072], P(None, 'ty', 'tx'), may hold values from -6 to 6
- wind_second: float32 [8, 768, 3072], P(None, 'ty', 'tx'), may hold values from -6 to 6
Outputs:
- thickness_new: float32 [8, 768, 3072], P(None, 'ty', 'tx')
- wind_first_new: float32 [8, 768, 3072], P(None, 'ty', 'tx')
- wind_second_new: float32 [8, 768, 3072], P(None, 'ty', 'tx')
Inputs may be any that keep to these rules, and one draw needn't show every extreme that they name: `dest_offset`: the intersections of one block name every one of the 4 distances at least 36 and at most 108 times, and one of them exactly 108 times. In every tx row some tile owner receives exactly 108 intersections from each of the 4 blocks that send to it. `slot_patch`: slots past the number of intersections that arrive from a sender receive nothing. The used slots of one tile owner name every one of its 144 patches at least once.
All inputs are finite; a program needn't handle non-finite values.
Results may differ from a plain program's by a relative error of at most 0.0003.
Values sent between devices are 32-bit elements; how exact they have to be, the bound alone decides.
A program may use at most 192 MiB of HBM per device.

v0:
```python
import jax
import jax.numpy as jnp
from jax import lax
from jax.sharding import PartitionSpec as P

PANELS = 4
STEPS = 4
TPATCH = 128


COURANT = 0.15
GRADIENT = 0.3


def from_behind(array, axis, by):
    size = lax.axis_size(axis)
    return lax.ppermute(array, axis, [(i, (i + by) % size) for i in range(size)])


def padded(cells, sides, width, closed):
    for axis, dim in sides:
        count = lax.axis_size(axis)
        ends = count if closed else count - 1
        head = lax.slice_in_dim(cells, 0, width, axis=dim)
        tail = lax.slice_in_dim(cells, cells.shape[dim] - width, cells.shape[dim], axis=dim)
        cells = jnp.concatenate(
            [
                lax.ppermute(tail, axis, [(i, (i + 1) % count) for i in range(ends)]),
                cells,
                lax.ppermute(head, axis, [((i + 1) % count, i) for i in range(ends)]),
            ],
            axis=dim,
        )
    return cells


def quarter_turn(code):
    cosine = (code == 0).astype(jnp.float32) - (code == 2).astype(jnp.float32)
    sine_value = (code == 1).astype(jnp.float32) - (code == 3).astype(jnp.float32)
    return (cosine, sine_value)


def advance(
    depth,
    cov_first,
    cov_second,
    con_first,
    con_second,
    depth_below,
    second_below,
    depth_above,
    second_above,
    depth_left,
    first_left,
    depth_right,
    first_right,
    wall_left,
    wall_right,
):
    face_below = 0.5 * (con_second + second_below)
    flux_below = jnp.maximum(face_below, 0.0) * depth_below + jnp.minimum(face_below, 0.0) * depth
    face_above = 0.5 * (con_second + second_above)
    flux_above = jnp.maximum(face_above, 0.0) * depth + jnp.minimum(face_above, 0.0) * depth_above
    face_left = 0.5 * (con_first + first_left) * wall_left
    flux_left = jnp.maximum(face_left, 0.0) * depth_left + jnp.minimum(face_left, 0.0) * depth
    face_right = 0.5 * (con_first + first_right) * wall_right
    flux_right = jnp.maximum(face_right, 0.0) * depth + jnp.minimum(face_right, 0.0) * depth_right
    new_depth = depth - COURANT * (flux_right - flux_left + (flux_above - flux_below))
    new_first = cov_first - GRADIENT * 0.5 * (depth_right - depth_left)
    new_second = cov_second - GRADIENT * 0.5 * (depth_above - depth_below)
    return (new_depth, new_first, new_second)


def rotation_codes(global_rows, total_rows, rotation):
    panel_rows = total_rows // PANELS
    panel = global_rows // panel_rows
    panel_iota = jnp.arange(PANELS, dtype=jnp.int32)
    matches = panel_iota[None, :] == panel[:, None]
    lower_code = jnp.sum(jnp.where(matches, rotation[0][None, :], 0), axis=1)
    upper_code = jnp.sum(jnp.where(matches, rotation[1][None, :], 0), axis=1)
    below_codes = jnp.where(global_rows % panel_rows == 0, lower_code, 0)
    above_codes = jnp.where(global_rows % panel_rows == panel_rows - 1, upper_code, 0)
    return (below_codes[:, None], above_codes[:, None])


def body(
    increments,
    remap_weights,
    dest_offset,
    slot_patch,
    rotation,
    basis,
    inv_metric_diag,
    inv_metric_cross,
    thickness,
    wind_first,
    wind_second,
):
    levels = thickness.shape[0]
    tile_rows = thickness.shape[1]
    tile_cols = thickness.shape[2]
    tx_count = lax.axis_size("tx")
    ty_count = lax.axis_size("ty")
    owners = slot_patch.shape[2]
    capacity = slot_patch.shape[3]
    patch_count = tile_rows * tile_cols // TPATCH
    row_width = 3 * levels * TPATCH
    tx_index = lax.axis_index("tx")
    ty_index = lax.axis_index("ty")
    partial_terms = jnp.einsum(
        "clsk,stpk->stclp", increments, remap_weights[0, 0], preferred_element_type=jnp.float32
    )
    entries = partial_terms.shape[0] * partial_terms.shape[1]
    partial_terms = partial_terms.reshape(entries, row_width)
    offsets = dest_offset.reshape(entries)
    onehot = (offsets[:, None] == jnp.arange(owners, dtype=jnp.int32)[None, :]).astype(jnp.int32)
    earlier = jnp.cumsum(onehot, axis=0) - onehot
    slot_index = jnp.sum(earlier * onehot, axis=1)
    position = offsets * capacity + slot_index
    outgoing = (
        jnp.zeros((owners * capacity, row_width), jnp.float32)
        .at[position]
        .set(partial_terms)
        .reshape(owners, capacity, row_width)
    )
    pieces = [outgoing[0]]
    for offset in range(1, owners):
        pieces.append(from_behind(outgoing[offset], "ty", offset))
    received = jnp.stack(pieces)
    patches = (
        jnp.zeros((patch_count, row_width), jnp.float32)
        .at[slot_patch.reshape(-1)]
        .add(received.reshape(-1, row_width))
    )
    blocks_per_row = tile_cols // TPATCH
    tiles = (
        patches.reshape(tile_rows, blocks_per_row, 3, levels, TPATCH)
        .transpose(2, 3, 0, 1, 4)
        .reshape(3, levels, tile_rows, tile_cols)
    )
    cov_first = wind_first + basis[0] * tiles[0] + basis[1] * tiles[1]
    cov_second = wind_second + basis[2] * tiles[0] + basis[3] * tiles[1]
    depth = thickness + tiles[2]
    total_rows = tile_rows * ty_count
    global_rows = ty_index * tile_rows + jnp.arange(tile_rows, dtype=jnp.int32)
    below_codes, above_codes = rotation_codes(global_rows, total_rows, rotation)
    cos_below, sin_below = quarter_turn(below_codes)
    cos_above, sin_above = quarter_turn(above_codes)
    col_iota = jnp.arange(tile_cols, dtype=jnp.int32)
    wall_left = jnp.where((tx_index == 0) & (col_iota == 0), 0.0, 1.0).astype(jnp.float32)
    wall_right = jnp.where(
        (tx_index == tx_count - 1) & (col_iota == tile_cols - 1), 0.0, 1.0
    ).astype(jnp.float32)
    for iteration in range(STEPS):
        con_first = inv_metric_diag[0] * cov_first + inv_metric_cross * cov_second
        con_second = inv_metric_cross * cov_first + inv_metric_diag[1] * cov_second
        row_ext = padded(jnp.stack([depth, con_first, con_second]), (("ty", 2),), 1, True)
        col_ext = padded(jnp.stack([depth, con_first]), (("tx", 3),), 1, False)
        lower = row_ext[:, :, :-2]
        upper = row_ext[:, :, 2:]
        second_below = sin_below * lower[1] + cos_below * lower[2]
        second_above = sin_above * upper[1] + cos_above * upper[2]
        depth, cov_first, cov_second = advance(
            depth,
            cov_first,
            cov_second,
            con_first,
            con_second,
            lower[0],
            second_below,
            upper[0],
            second_above,
            col_ext[0, :, :, :-2],
            col_ext[1, :, :, :-2],
            col_ext[0, :, :, 2:],
            col_ext[1, :, :, 2:],
            wall_left,
            wall_right,
        )
    return (depth, cov_first, cov_second)


def solution(mesh):
    in_specs = (
        P(None, None, "tx", "ty"),
        P("tx", "ty", None, None, None, None),
        P("tx", "ty", None, None),
        P("tx", "ty", None, None),
        P(),
        P(None, "ty", "tx"),
        P(None, "ty", "tx"),
        P("ty", "tx"),
        P(None, "ty", "tx"),
        P(None, "ty", "tx"),
        P(None, "ty", "tx"),
    )
    out_specs = (P(None, "ty", "tx"), P(None, "ty", "tx"), P(None, "ty", "tx"))
    return jax.shard_map(body, mesh=mesh, in_specs=in_specs, out_specs=out_specs, check_vma=False)
```

profile of v0, /device:TPU:1, one launch (start us, length us, event | category | flops | bytes accessed | tf_op | source)
XLA Modules:
  0.0 221.9 jit_solution(7453993708558658296)
XLA Ops:
  4.4 10.7 %fusion.4 = f32[144,2,3,8,128]{4,3,2,1,0:T(8,128)} fusion(bf16[1,1,144,2,128,256]{5,4,3,2,1,0:T(8,128)(2,1)} %param.12, bf16[3,8,144,256,1]{3,2,1,0,4:T(8,128)(2,1)S(1)} %bitcast.408), kind=kOutput, calls=%fused_computation.7 | convolution fusion | flops 452984832 | bytes 24182784 | tf_op jit(solution)/shard_map/clsk,stpk->stclp/dot_general | solution.py:110
  15.1 4.8 %reshape.214 = f32[288,3072]{1,0:T(8,128)} reshape(f32[144,2,3,8,128]{4,3,2,1,0:T(8,128)} %fusion.4) | data formatting | bytes 7077888 | tf_op jit(solution)/shard_map/reshape | solution.py:114
  19.9 6.7 %scatter_custom_fusion = f32[432,3072]{1,0:T(8,128)} fusion(s32[288]{0:T(512)S(1)} %fusion.94, f32[288,3072]{1,0:T(8,128)} %reshape.214, f32[]{:T(128)} %constant.21.clone.1), kind=kCustom, calls=%fused_computation.5 | custom fusion | bytes 5308928 | tf_op jit(solution)/shard_map/scatter | solution.py:123
  26.6 4.9 %slice_bitcast_fusion = (f32[1,108,3072]{2,1,0:T(8,128)S(1)}, f32[108,3072]{1,0:T(8,128)}, f32[108,3072]{1,0:T(8,128)}, f32[108,3072]{1,0:T(8,128)S(1)}) fusion(f32[432,3072]{1,0:T(8,128)} %scatter_custom_fusion), kind=kLoop, calls=%fused_computation.9 | loop fusion | bytes 10616832 | tf_op jit(solution)/shard_map/slice | solution.py:126
  31.5 3.6 %collective-permute-start.1 = (f32[108,3072]{1,0:T(8,128)}, f32[108,3072]{1,0:T(8,128)}, u32[]{:S(2)}, u32[]{:S(2)}) collective-permute-start(f32[108,3072]{1,0:T(8,128)} %get-tuple-element.19), channel_id=1, source_target_pairs={{0,2},{1,3},{2,4},{3,5},{4,6},{5,7},{6,8},{7,9},{8,10},{9,11},{10,... | collective-permute-start | bytes 3981320 | tf_op jit(solution)/shard_map/ppermute | solution.py:17
  35.1 2.2 collective-permute-start.2
  38.9 29.9 %collective-permute-done.1 = f32[108,3072]{1,0:T(8,128)} collective-permute-done((f32[108,3072]{1,0:T(8,128)}, f32[108,3072]{1,0:T(8,128)}, u32[]{:S(2)}, u32[]{:S(2)}) %collective-permute-start.1) | collective-permute-done | bytes 1327136 | tf_op jit(solution)/shard_map/ppermute | solution.py:17
  68.8 58.6 %collective-permute-done.2 = f32[108,3072]{1,0:T(8,128)} collective-permute-done((f32[108,3072]{1,0:T(8,128)}, f32[108,3072]{1,0:T(8,128)}, u32[]{:S(2)}, u32[]{:S(2)}) %collective-permute-start.2) | collective-permute-done | bytes 1327136 | tf_op jit(solution)/shard_map/ppermute | solution.py:17
  127.4 5.2 %pad_maximum_fusion = f32[4,108,3072]{2,1,0:T(8,128)} fusion(f32[1,108,3072]{2,1,0:T(8,128)} %bitcast.11, f32[1,108,3072]{2,1,0:T(8,128)} %bitcast.10, f32[1,108,3072]{2,1,0:T(8,128)} %bitcast.9, f32[1,108,3072]{2,1,0:T(8,128)S(1)} %get-tuple-element.17), kind=kLoop, calls=%fused_computation.4 | loop fusion | flops 3981312 | bytes 10616832 | tf_op jit(solution)/shard_map/stack | solution.py:129
  132.7 4.4 %reshape.222 = f32[432,3072]{1,0:T(8,128)} reshape(f32[4,108,3072]{2,1,0:T(8,128)} %pad_maximum_fusion) | data formatting | bytes 10616832 | tf_op jit(solution)/shard_map/reshape | solution.py:133
  137.1 9.8 %scatter_custom_fusion.1 = f32[144,3072]{1,0:T(8,128)S(1)} fusion(s32[432]{0:T(512)S(1)} %bitcast.429, f32[432,3072]{1,0:T(8,128)} %reshape.222, f32[]{:T(128)} %constant.21.clone.1), kind=kCustom, calls=%fused_computation.10 | custom fusion | flops 1327104 | bytes 1769984 | tf_op jit(solution)/shard_map/scatter-add | solution.py:133
  151.0 1.5 fusion.82
  153.0 1.5 collective-permute-start.6
  154.4 4.0 %collective-permute-start.3 = (f32[2,8,48,1]{3,2,1,0:T(8,128)S(1)}, f32[2,8,48,1]{3,2,1,0:T(8,128)S(1)}, u32[]{:S(2)}, u32[]{:S(2)}) collective-permute-start(f32[2,8,48,1]{3,2,1,0:T(8,128)S(1)} %get-tuple-element.40), channel_id=1, source_target_pairs={{16,0},{32,16},{48,32},{64,48},{80,64},{96,80},{112,96},{17,1},{33... | collective-permute-start | bytes 9224 | tf_op jit(solution)/shard_map/ppermute | solution.py:30
  158.4 3.3 %collective-permute-start.4 = (f32[2,8,48,1]{3,2,1,0:T(8,128)S(1)}, f32[2,8,48,1]{3,2,1,0:T(8,128)S(1)}, u32[]{:S(2)}, u32[]{:S(2)}) collective-permute-start(f32[2,8,48,1]{3,2,1,0:T(8,128)S(1)} %get-tuple-element.41), channel_id=1, source_target_pairs={{0,16},{16,32},{32,48},{48,64},{64,80},{80,96},{96,112},{1,17},{17... | collective-permute-start | bytes 9224 | tf_op jit(solution)/shard_map/ppermute | solution.py:28
  161.8 3.3 %collective-permute-done.3 = f32[2,8,48,1]{3,2,1,0:T(8,128)S(1)} collective-permute-done((f32[2,8,48,1]{3,2,1,0:T(8,128)S(1)}, f32[2,8,48,1]{3,2,1,0:T(8,128)S(1)}, u32[]{:S(2)}, u32[]{:S(2)}) %collective-permute-start.3) | collective-permute-done | bytes 3104 | tf_op jit(solution)/shard_map/ppermute | solution.py:30
  166.8 1.8 multiply_subtract_fusion.11
  168.7 4.8 %collective-permute-start.9 = (f32[3,8,1,384]{3,2,1,0:T(1,128)S(1)}, f32[3,8,1,384]{3,2,1,0:T(1,128)S(1)}, u32[]{:S(2)}, u32[]{:S(2)}) collective-permute-start(f32[3,8,1,384]{3,2,1,0:T(1,128)S(1)} %get-tuple-element.25), channel_id=1, source_target_pairs={{1,0},{2,1},{3,2},{4,3},{5,4},{6,5},{7,6},{8,7},{9,8},{10,9},{11,1... | collective-permute-start | bytes 110600 | tf_op jit(solution)/shard_map/ppermute | solution.py:30
  173.7 1.9 collective-permute-start.7
  175.6 4.9 %collective-permute-start.8 = (f32[2,8,48,1]{3,2,1,0:T(8,128)S(1)}, f32[2,8,48,1]{3,2,1,0:T(8,128)S(1)}, u32[]{:S(2)}, u32[]{:S(2)}) collective-permute-start(f32[2,8,48,1]{3,2,1,0:T(8,128)S(1)} %get-tuple-element.39), channel_id=1, source_target_pairs={{0,16},{16,32},{32,48},{48,64},{64,80},{80,96},{96,112},{1,17},{17... | collective-permute-start | bytes 9224 | tf_op jit(solution)/shard_map/ppermute | solution.py:28
  180.6 3.5 %collective-permute-done.7 = f32[2,8,48,1]{3,2,1,0:T(8,128)S(1)} collective-permute-done((f32[2,8,48,1]{3,2,1,0:T(8,128)S(1)}, f32[2,8,48,1]{3,2,1,0:T(8,128)S(1)}, u32[]{:S(2)}, u32[]{:S(2)}) %collective-permute-start.7) | collective-permute-done | bytes 3104 | tf_op jit(solution)/shard_map/ppermute | solution.py:30
  185.8 1.8 multiply_subtract_fusion.8
  187.8 1.5 collective-permute-start.14
  189.4 1.9 collective-permute-start.11
  191.3 4.9 %collective-permute-start.12 = (f32[2,8,48,1]{3,2,1,0:T(8,128)S(1)}, f32[2,8,48,1]{3,2,1,0:T(8,128)S(1)}, u32[]{:S(2)}, u32[]{:S(2)}) collective-permute-start(f32[2,8,48,1]{3,2,1,0:T(8,128)S(1)} %get-tuple-element.37), channel_id=1, source_target_pairs={{0,16},{16,32},{32,48},{48,64},{64,80},{80,96},{96,112},{1,17},{17... | collective-permute-start | bytes 9224 | tf_op jit(solution)/shard_map/ppermute | solution.py:28
  196.3 3.5 %collective-permute-done.11 = f32[2,8,48,1]{3,2,1,0:T(8,128)S(1)} collective-permute-done((f32[2,8,48,1]{3,2,1,0:T(8,128)S(1)}, f32[2,8,48,1]{3,2,1,0:T(8,128)S(1)}, u32[]{:S(2)}, u32[]{:S(2)}) %collective-permute-start.11) | collective-permute-done | bytes 3104 | tf_op jit(solution)/shard_map/ppermute | solution.py:30
  201.6 1.8 multiply_subtract_fusion.5
  203.4 3.2 %collective-permute-start.17 = (f32[3,8,1,384]{3,2,1,0:T(1,128)S(1)}, f32[3,8,1,384]{3,2,1,0:T(1,128)S(1)}, u32[]{:S(2)}, u32[]{:S(2)}) collective-permute-start(f32[3,8,1,384]{3,2,1,0:T(1,128)S(1)} %get-tuple-element.21), channel_id=1, source_target_pairs={{1,0},{2,1},{3,2},{4,3},{5,4},{6,5},{7,6},{8,7},{9,8},{10,9},{11,1... | collective-permute-start | bytes 110600 | tf_op jit(solution)/shard_map/ppermute | solution.py:30
  206.7 1.9 collective-permute-start.15
  208.7 4.7 %collective-permute-start.16 = (f32[2,8,48,1]{3,2,1,0:T(8,128)S(1)}, f32[2,8,48,1]{3,2,1,0:T(8,128)S(1)}, u32[]{:S(2)}, u32[]{:S(2)}) collective-permute-start(f32[2,8,48,1]{3,2,1,0:T(8,128)S(1)} %get-tuple-element.35), channel_id=1, source_target_pairs={{0,16},{16,32},{32,48},{48,64},{64,80},{80,96},{96,112},{1,17},{17... | collective-permute-start | bytes 9224 | tf_op jit(solution)/shard_map/ppermute | solution.py:28
  213.3 3.5 %collective-permute-done.15 = f32[2,8,48,1]{3,2,1,0:T(8,128)S(1)} collective-permute-done((f32[2,8,48,1]{3,2,1,0:T(8,128)S(1)}, f32[2,8,48,1]{3,2,1,0:T(8,128)S(1)}, u32[]{:S(2)}, u32[]{:S(2)}) %collective-permute-start.15) | collective-permute-done | bytes 3104 | tf_op jit(solution)/shard_map/ppermute | solution.py:30
  219.5 2.4 %multiply_subtract_fusion.2 = f32[8,48,384]{2,1,0:T(8,128)} fusion(f32[8,48,384]{2,1,0:T(8,128)S(1)} %multiply_subtract_fusion.5, f32[1,8,48,384]{3,2,1,0:T(8,128)S(1)} %fusion.89, f32[1,8,48,384]{3,2,1,0:T(8,128)S(1)} %get-tuple-element.5, f32[1,8,48,384]{3,2,1,0:T(8,128)S(1)} %bitcast.412, f32[3,8,1,384]{3,2,1,0:T(1,128)S(1)} %collective-permute-done.18, ...), kind=kLoop, calls=%fused_computation.150 | loop fusion | flops 10469376 | bytes 4433664 | tf_op jit(solution)/shard_map/sub | solution.py:68
  (94 shorter events, 18.5 us)
Async XLA Ops:
  0.6 3.8 %copy-start = (bf16[3,8,144,256]{3,2,1,0:T(8,128)(2,1)S(1)}, bf16[3,8,144,256]{3,2,1,0:T(8,128)(2,1)}, u32[]{:S(2)}) copy-start(bf16[3,8,144,256]{3,2,1,0:T(8,128)(2,1)} %param.11) | copy-start | bytes 5308420
  26.6 11.3 %copy-start.12 = (s32[1,1,4,108]{3,2,1,0:T(4,128)S(1)}, s32[1,1,4,108]{3,2,1,0:T(4,128)}, u32[]{:S(2)}) copy-start(s32[1,1,4,108]{3,2,1,0:T(4,128)} %param.14) | copy-start | bytes 5188
  26.6 11.4 %copy-start.13 = (s32[2,4]{1,0:T(2,128)S(1)}, s32[2,4]{1,0:T(2,128)}, u32[]{:S(2)}) copy-start(s32[2,4]{1,0:T(2,128)} %param.15) | copy-start | bytes 100
  26.6 11.5 %copy-start.6 = (f32[4,48,384]{2,1,0:T(8,128)S(1)}, f32[4,48,384]{2,1,0:T(8,128)}, u32[]{:S(2)}) copy-start(f32[4,48,384]{2,1,0:T(8,128)} %param.16) | copy-start | bytes 884740
  26.6 11.5 %copy-start.11 = (f32[2,48,384]{2,1,0:T(8,128)S(1)}, f32[2,48,384]{2,1,0:T(8,128)}, u32[]{:S(2)}) copy-start(f32[2,48,384]{2,1,0:T(8,128)} %param.17) | copy-start | bytes 442372
  31.5 37.3 %collective-permute-start.1 = (f32[108,3072]{1,0:T(8,128)}, f32[108,3072]{1,0:T(8,128)}, u32[]{:S(2)}, u32[]{:S(2)}) collective-permute-start(f32[108,3072]{1,0:T(8,128)} %get-tuple-element.19), channel_id=1, source_target_pairs={{0,2},{1,3},{2,4},{3,5},{4,6},{5,7},{6,8},{7,9},{8,10},{9,11},{10,... | collective-permute-start | bytes 3981320 | tf_op jit(solution)/shard_map/ppermute | solution.py:17
  35.1 92.3 %collective-permute-start.2 = (f32[108,3072]{1,0:T(8,128)}, f32[108,3072]{1,0:T(8,128)}, u32[]{:S(2)}, u32[]{:S(2)}) collective-permute-start(f32[108,3072]{1,0:T(8,128)} %get-tuple-element.18), channel_id=1, source_target_pairs={{0,3},{1,4},{2,5},{3,6},{4,7},{5,8},{6,9},{7,10},{8,11},{9,12},{10... | collective-permute-start | bytes 3981320 | tf_op jit(solution)/shard_map/ppermute | solution.py:17
  37.3 90.1 %collective-permute-start = (f32[108,3072]{1,0:T(8,128)S(1)}, f32[108,3072]{1,0:T(8,128)}, u32[]{:S(2)}, u32[]{:S(2)}) collective-permute-start(f32[108,3072]{1,0:T(8,128)S(1)} %get-tuple-element.20), channel_id=1, source_target_pairs={{0,1},{1,2},{2,3},{3,4},{4,5},{5,6},{6,7},{7,8},{8,9},{9,10},{10,1... | collective-permute-start | bytes 3981320 | tf_op jit(solution)/shard_map/ppermute | solution.py:17
  148.7 2.3 %copy-start.2 = (f32[48,384]{1,0:T(8,128)S(1)}, f32[48,384]{1,0:T(8,128)}, u32[]{:S(2)}) copy-start(f32[48,384]{1,0:T(8,128)} %param.18) | copy-start | bytes 221188
  148.7 2.3 %copy-start.4 = (f32[48,384]{1,0:T(8,128)S(1)}, f32[48,384]{1,0:T(8,128)}, u32[]{:S(2)}) copy-start(f32[48,384]{1,0:T(8,128)} %get-tuple-element.47) | copy-start | bytes 221188
  148.7 2.3 %copy-start.7 = (f32[48,384]{1,0:T(8,128)S(1)}, f32[48,384]{1,0:T(8,128)}, u32[]{:S(2)}) copy-start(f32[48,384]{1,0:T(8,128)} %get-tuple-element.54) | copy-start | bytes 221188
  148.7 2.3 %copy-start.8 = (f32[48,384]{1,0:T(8,128)S(1)}, f32[48,384]{1,0:T(8,128)}, u32[]{:S(2)}) copy-start(f32[48,384]{1,0:T(8,128)} %get-tuple-element.55) | copy-start | bytes 221188
  148.7 2.3 %copy-start.9 = (f32[48,384]{1,0:T(8,128)S(1)}, f32[48,384]{1,0:T(8,128)}, u32[]{:S(2)}) copy-start(f32[48,384]{1,0:T(8,128)} %get-tuple-element.56) | copy-start | bytes 221188
  148.7 2.3 %copy-start.10 = (f32[48,384]{1,0:T(8,128)S(1)}, f32[48,384]{1,0:T(8,128)}, u32[]{:S(2)}) copy-start(f32[48,384]{1,0:T(8,128)} %get-tuple-element.57) | copy-start | bytes 221188
  151.0 1.7 copy-start.3
  152.9 13.4 %collective-permute-start.5 = (f32[3,8,1,384]{3,2,1,0:T(1,128)S(1)}, f32[3,8,1,384]{3,2,1,0:T(1,128)S(1)}, u32[]{:S(2)}, u32[]{:S(2)}) collective-permute-start(f32[3,8,1,384]{3,2,1,0:T(1,128)S(1)} %get-tuple-element.27), channel_id=1, source_target_pairs={{1,0},{2,1},{3,2},{4,3},{5,4},{6,5},{7,6},{8,7},{9,8},{10,9},{11,1... | collective-permute-start | bytes 110600 | tf_op jit(solution)/shard_map/ppermute | solution.py:30
  153.0 13.3 %collective-permute-start.6 = (f32[3,8,1,384]{3,2,1,0:T(1,128)S(1)}, f32[3,8,1,384]{3,2,1,0:T(1,128)S(1)}, u32[]{:S(2)}, u32[]{:S(2)}) collective-permute-start(f32[3,8,1,384]{3,2,1,0:T(1,128)S(1)} %get-tuple-element.28), channel_id=1, source_target_pairs={{0,1},{1,2},{2,3},{3,4},{4,5},{5,6},{6,7},{7,8},{8,9},{9,10},{10,1... | collective-permute-start | bytes 110600 | tf_op jit(solution)/shard_map/ppermute | solution.py:28
  154.4 10.7 %collective-permute-start.3 = (f32[2,8,48,1]{3,2,1,0:T(8,128)S(1)}, f32[2,8,48,1]{3,2,1,0:T(8,128)S(1)}, u32[]{:S(2)}, u32[]{:S(2)}) collective-permute-start(f32[2,8,48,1]{3,2,1,0:T(8,128)S(1)} %get-tuple-element.40), channel_id=1, source_target_pairs={{16,0},{32,16},{48,32},{64,48},{80,64},{96,80},{112,96},{17,1},{33... | collective-permute-start | bytes 9224 | tf_op jit(solution)/shard_map/ppermute | solution.py:30
  158.4 7.8 %collective-permute-start.4 = (f32[2,8,48,1]{3,2,1,0:T(8,128)S(1)}, f32[2,8,48,1]{3,2,1,0:T(8,128)S(1)}, u32[]{:S(2)}, u32[]{:S(2)}) collective-permute-start(f32[2,8,48,1]{3,2,1,0:T(8,128)S(1)} %get-tuple-element.41), channel_id=1, source_target_pairs={{0,16},{16,32},{32,48},{48,64},{64,80},{80,96},{96,112},{1,17},{17... | collective-permute-start | bytes 9224 | tf_op jit(solution)/shard_map/ppermute | solution.py:28
  168.7 16.6 %collective-permute-start.10 = (f32[3,8,1,384]{3,2,1,0:T(1,128)S(1)}, f32[3,8,1,384]{3,2,1,0:T(1,128)S(1)}, u32[]{:S(2)}, u32[]{:S(2)}) collective-permute-start(f32[3,8,1,384]{3,2,1,0:T(1,128)S(1)} %get-tuple-element.26), channel_id=1, source_target_pairs={{0,1},{1,2},{2,3},{3,4},{4,5},{5,6},{6,7},{7,8},{8,9},{9,10},{10,1... | collective-permute-start | bytes 110600 | tf_op jit(solution)/shard_map/ppermute | solution.py:28
  168.7 16.5 %collective-permute-start.9 = (f32[3,8,1,384]{3,2,1,0:T(1,128)S(1)}, f32[3,8,1,384]{3,2,1,0:T(1,128)S(1)}, u32[]{:S(2)}, u32[]{:S(2)}) collective-permute-start(f32[3,8,1,384]{3,2,1,0:T(1,128)S(1)} %get-tuple-element.25), channel_id=1, source_target_pairs={{1,0},{2,1},{3,2},{4,3},{5,4},{6,5},{7,6},{8,7},{9,8},{10,9},{11,1... | collective-permute-start | bytes 110600 | tf_op jit(solution)/shard_map/ppermute | solution.py:30
  173.7 10.4 %collective-permute-start.7 = (f32[2,8,48,1]{3,2,1,0:T(8,128)S(1)}, f32[2,8,48,1]{3,2,1,0:T(8,128)S(1)}, u32[]{:S(2)}, u32[]{:S(2)}) collective-permute-start(f32[2,8,48,1]{3,2,1,0:T(8,128)S(1)} %get-tuple-element.38), channel_id=1, source_target_pairs={{16,0},{32,16},{48,32},{64,48},{80,64},{96,80},{112,96},{17,1},{33... | collective-permute-start | bytes 9224 | tf_op jit(solution)/shard_map/ppermute | solution.py:30
  175.6 9.7 %collective-permute-start.8 = (f32[2,8,48,1]{3,2,1,0:T(8,128)S(1)}, f32[2,8,48,1]{3,2,1,0:T(8,128)S(1)}, u32[]{:S(2)}, u32[]{:S(2)}) collective-permute-start(f32[2,8,48,1]{3,2,1,0:T(8,128)S(1)} %get-tuple-element.39), channel_id=1, source_target_pairs={{0,16},{16,32},{32,48},{48,64},{64,80},{80,96},{96,112},{1,17},{17... | collective-permute-start | bytes 9224 | tf_op jit(solution)/shard_map/ppermute | solution.py:28
  187.7 13.3 %collective-permute-start.13 = (f32[3,8,1,384]{3,2,1,0:T(1,128)S(1)}, f32[3,8,1,384]{3,2,1,0:T(1,128)S(1)}, u32[]{:S(2)}, u32[]{:S(2)}) collective-permute-start(f32[3,8,1,384]{3,2,1,0:T(1,128)S(1)} %get-tuple-element.23), channel_id=1, source_target_pairs={{1,0},{2,1},{3,2},{4,3},{5,4},{6,5},{7,6},{8,7},{9,8},{10,9},{11,1... | collective-permute-start | bytes 110600 | tf_op jit(solution)/shard_map/ppermute | solution.py:30
  187.8 13.2 %collective-permute-start.14 = (f32[3,8,1,384]{3,2,1,0:T(1,128)S(1)}, f32[3,8,1,384]{3,2,1,0:T(1,128)S(1)}, u32[]{:S(2)}, u32[]{:S(2)}) collective-permute-start(f32[3,8,1,384]{3,2,1,0:T(1,128)S(1)} %get-tuple-element.24), channel_id=1, source_target_pairs={{0,1},{1,2},{2,3},{3,4},{4,5},{5,6},{6,7},{7,8},{8,9},{9,10},{10,1... | collective-permute-start | bytes 110600 | tf_op jit(solution)/shard_map/ppermute | solution.py:28
  189.4 10.4 %collective-permute-start.11 = (f32[2,8,48,1]{3,2,1,0:T(8,128)S(1)}, f32[2,8,48,1]{3,2,1,0:T(8,128)S(1)}, u32[]{:S(2)}, u32[]{:S(2)}) collective-permute-start(f32[2,8,48,1]{3,2,1,0:T(8,128)S(1)} %get-tuple-element.36), channel_id=1, source_target_pairs={{16,0},{32,16},{48,32},{64,48},{80,64},{96,80},{112,96},{17,1},{33... | collective-permute-start | bytes 9224 | tf_op jit(solution)/shard_map/ppermute | solution.py:30
  191.3 9.7 %collective-permute-start.12 = (f32[2,8,48,1]{3,2,1,0:T(8,128)S(1)}, f32[2,8,48,1]{3,2,1,0:T(8,128)S(1)}, u32[]{:S(2)}, u32[]{:S(2)}) collective-permute-start(f32[2,8,48,1]{3,2,1,0:T(8,128)S(1)} %get-tuple-element.37), channel_id=1, source_target_pairs={{0,16},{16,32},{32,48},{48,64},{64,80},{80,96},{96,112},{1,17},{17... | collective-permute-start | bytes 9224 | tf_op jit(solution)/shard_map/ppermute | solution.py:28
  203.4 14.7 %collective-permute-start.17 = (f32[3,8,1,384]{3,2,1,0:T(1,128)S(1)}, f32[3,8,1,384]{3,2,1,0:T(1,128)S(1)}, u32[]{:S(2)}, u32[]{:S(2)}) collective-permute-start(f32[3,8,1,384]{3,2,1,0:T(1,128)S(1)} %get-tuple-element.21), channel_id=1, source_target_pairs={{1,0},{2,1},{3,2},{4,3},{5,4},{6,5},{7,6},{8,7},{9,8},{10,9},{11,1... | collective-permute-start | bytes 110600 | tf_op jit(solution)/shard_map/ppermute | solution.py:30
  206.6 11.5 %collective-permute-start.18 = (f32[3,8,1,384]{3,2,1,0:T(1,128)S(1)}, f32[3,8,1,384]{3,2,1,0:T(1,128)S(1)}, u32[]{:S(2)}, u32[]{:S(2)}) collective-permute-start(f32[3,8,1,384]{3,2,1,0:T(1,128)S(1)} %get-tuple-element.22), channel_id=1, source_target_pairs={{0,1},{1,2},{2,3},{3,4},{4,5},{5,6},{6,7},{7,8},{8,9},{9,10},{10,1... | collective-permute-start | bytes 110600 | tf_op jit(solution)/shard_map/ppermute | solution.py:28
  206.7 10.1 %collective-permute-start.15 = (f32[2,8,48,1]{3,2,1,0:T(8,128)S(1)}, f32[2,8,48,1]{3,2,1,0:T(8,128)S(1)}, u32[]{:S(2)}, u32[]{:S(2)}) collective-permute-start(f32[2,8,48,1]{3,2,1,0:T(8,128)S(1)} %get-tuple-element.34), channel_id=1, source_target_pairs={{16,0},{32,16},{48,32},{64,48},{80,64},{96,80},{112,96},{17,1},{33... | collective-permute-start | bytes 9224 | tf_op jit(solution)/shard_map/ppermute | solution.py:30
  208.7 9.4 %collective-permute-start.16 = (f32[2,8,48,1]{3,2,1,0:T(8,128)S(1)}, f32[2,8,48,1]{3,2,1,0:T(8,128)S(1)}, u32[]{:S(2)}, u32[]{:S(2)}) collective-permute-start(f32[2,8,48,1]{3,2,1,0:T(8,128)S(1)} %get-tuple-element.35), channel_id=1, source_target_pairs={{0,16},{16,32},{32,48},{48,64},{64,80},{80,96},{96,112},{1,17},{17... | collective-permute-start | bytes 9224 | tf_op jit(solution)/shard_map/ppermute | solution.py:28
  218.0 3.9 %copy-start.1 = (bf16[3,8,144,256]{3,2,1,0:T(8,128)(2,1)S(1)}, bf16[3,8,144,256]{3,2,1,0:T(8,128)(2,1)}, u32[]{:S(2)}) copy-start(bf16[3,8,144,256]{3,2,1,0:T(8,128)(2,1)} %param.11) | copy-start | bytes 5308420
  (1 other events, 1.1 us)
where the time goes:
time: 222 us
  waiting for transfers between devices  107 us (48%)
  starting transfers between devices  45.2 us (20%)
  other arithmetic  31.9 us (14%)
  local copies, waits for them, and re-layouts  26 us (12%)
  matrix products  10.7 us (5%)
    ppermute x3, waiting for transfers between devices, from_behind(): lax.ppermute(array, axis, [(i, (i + by) % size) for i in range(size)])  88.5 us
    ppermute x8, starting transfers between devices, padded(): lax.ppermute(tail, axis, [(i, (i + 1) % count) for i in range(ends)])  20.9 us
    ppermute x8, starting transfers between devices, padded(): lax.ppermute(head, axis, [((i + 1) % count, i) for i in range(ends)])  17.9 us
    ppermute x8, waiting for transfers between devices, padded(): lax.ppermute(head, axis, [((i + 1) % count, i) for i in range(ends)])  13.8 us
    dot_general x1, matrix products, body(): jnp.einsum('clsk,stpk->stclp', increments, remap_weights[0, 0], preferred...  10.7 us
    scatter-add x1, other arithmetic, body(): patches = jnp.zeros((patch_count, row_width), jnp.float32).at[slot_patch....  9.81 us
    sub x4, other arithmetic, advance(): depth - COURANT * (flux_right - flux_left + (flux_above - flux_below))  7.7 us
    scatter x1, local copies, waits for them, and re-layouts, body(): outgoing = jnp.zeros((owners * capacity, row_width), jnp.float32).at[posi...  6.67 us
  transfers between devices with their start and end apart: 19, of which 10 were waited for; matrix products, arithmetic and copies ran while one was open for 1% of the time, Pallas kernels for 0%

commit v1 on v0

v1 whole, which is shorter than its diff:
```python
import jax
import jax.numpy as jnp
from jax import lax
from jax.experimental import pallas as pl
from jax.experimental.pallas import tpu as pltpu
from jax.sharding import PartitionSpec as P

MESH = pl.DeviceIdType.MESH
PANELS = 4
STEPS = 4
HALO = 4
COURANT = 0.15
HALF_GRADIENT = 0.15
LANES = 128
GROUPS = 32
NX = 4
SEND_CHUNKS = 6
W_SLOTS = 4
W_ROWS = 16


def kernel(
    perm, prev, last, turn, inc, wts, basis, diag, cross, depth_in, first_in, second_in,
    out_depth, out_first, out_second,
    wbuf, inc_v, half0, half1, term, send, recv, relay, acc, xa, xb, metric, bases,
    state_in, out_v, grid_raw, grid_side, basis_raw, packed, strips,
    w_sem, in_sem, field_sem, out_sem, send_sem, recv_sem, relay_send_sem, relay_recv_sem,
    grid_send_sem, grid_recv_sem, halo_send_sem, halo_recv_sem,
):
    tx = lax.axis_index("tx")
    ty = lax.axis_index("ty")
    n_tx = lax.axis_size("tx")
    n_ty = lax.axis_size("ty")
    x = lax.rem(ty, NX)
    odd = lax.rem(tx, 2) == 1
    flows, capacity = send.shape[0], send.shape[1]
    entries = term.shape[0] - 1
    slots = acc.shape[0] - 1
    per = capacity // SEND_CHUNKS
    rows = state_in.shape[3]
    levels = state_in.shape[2]
    blocks = state_in.shape[1]
    w_chunks = wts.shape[0] // W_ROWS

    def dev(dx, dy):
        return (lax.rem(tx + dx + n_tx, n_tx), lax.rem(ty + dy + n_ty, n_ty))

    barrier = pltpu.get_barrier_semaphore()
    partners = [(0, s * d) for d in (1, 2, 3, 4) for s in (1, -1)]
    partners += [(s, d) for s in (1, -1) for d in (-1, 0, 1)]
    for dx, dy in partners:
        pl.semaphore_signal(barrier, inc=1, device_id=dev(dx, dy), device_id_type=MESH)

    def w_copy(chunk, slot):
        return pltpu.make_async_copy(wts.at[pl.ds(chunk * W_ROWS, W_ROWS)], wbuf.at[slot], w_sem.at[slot])

    inc_copy = pltpu.make_async_copy(inc, inc_v, in_sem)
    inc_copy.start()
    for slot in range(W_SLOTS):
        w_copy(slot, slot).start()
    field_copies = [
        pltpu.make_async_copy(diag, grid_raw.at[0:2, 8 : 8 + rows], field_sem.at[0]),
        pltpu.make_async_copy(cross, grid_raw.at[2, 8 : 8 + rows], field_sem.at[1]),
        pltpu.make_async_copy(basis, basis_raw, field_sem.at[2]),
    ]
    for i, field in enumerate((depth_in, first_in, second_in)):
        for b in range(blocks):
            field_copies.append(
                pltpu.make_async_copy(
                    field.at[:, :, b * LANES : (b + 1) * LANES], state_in.at[i, b], field_sem.at[3 + i * blocks + b]
                )
            )
    for copy in field_copies:
        copy.start()

    zero_row = jnp.zeros(term.shape[1:], jnp.float32)
    term[entries] = zero_row
    acc[slots] = zero_row

    inc_copy.wait()

    def term_chunk(chunk, carry):
        slot = lax.rem(chunk, W_SLOTS)
        start = pl.multiple_of(chunk * W_ROWS, W_ROWS)
        cells = inc_v[:, pl.ds(start, W_ROWS), :].astype(jnp.float32)
        pairs = cells.shape[0]
        half0[...] = cells[:, :, :LANES].reshape(pairs * W_ROWS, LANES)
        half1[...] = cells[:, :, LANES:].reshape(pairs * W_ROWS, LANES)
        w_copy(chunk, slot).wait()
        for s in range(W_ROWS):
            lhs = jnp.concatenate(
                [half0[pl.ds(s, pairs, stride=W_ROWS), :], half1[pl.ds(s, pairs, stride=W_ROWS), :]], axis=1
            ).astype(jnp.bfloat16)
            product = lax.dot_general(
                lhs, wbuf[slot, s], (((1,), (1,)), ((), ())), preferred_element_type=jnp.float32
            )
            entry = 2 * (start + s)
            term[entry] = product[:, :LANES]
            term[entry + 1] = product[:, LANES:]

        @pl.when(chunk + W_SLOTS < w_chunks)
        def _():
            w_copy(chunk + W_SLOTS, slot).start()

        return carry

    lax.fori_loop(0, w_chunks, term_chunk, 0)

    pl.semaphore_wait(barrier, len(partners))

    def direct(d, c):
        part = pl.ds(c * per, per)
        return pltpu.make_async_remote_copy(
            send.at[d - 1, part], recv.at[d - 1, part], send_sem.at[d - 1, c], recv_sem.at[d - 1, c],
            device_id=dev(0, d), device_id_type=MESH,
        )

    def first_leg(d, c):
        part = pl.ds(c * per, per)
        return pltpu.make_async_remote_copy(
            send.at[d - 1, part], relay.at[d - 1, part], send_sem.at[d - 1, c], relay_recv_sem.at[d - 1, c],
            device_id=dev(0, NX), device_id_type=MESH,
        )

    def second_leg(d, c):
        part = pl.ds(c * per, per)
        return pltpu.make_async_remote_copy(
            relay.at[d - 1, part], recv.at[d - 1, part], relay_send_sem.at[d - 1, c], recv_sem.at[d - 1, c],
            device_id=dev(0, d - NX), device_id_type=MESH,
        )

    def relayed(d):
        return jnp.logical_and(odd, x + d >= NX)

    def send_chunk(c, carry):
        for d in range(1, flows + 1):

            def gather(i, inner):
                k = c * per + i
                send[d - 1, k] = term[perm[d * capacity + k]]
                return inner

            lax.fori_loop(0, per, gather, 0, unroll=6)

            @pl.when(relayed(d))
            def _():
                first_leg(d, c).start()

            @pl.when(jnp.logical_not(relayed(d)))
            def _():
                direct(d, c).start()

        return carry

    lax.fori_loop(0, SEND_CHUNKS, send_chunk, 0)

    for copy in field_copies:
        copy.wait()

    own = slice(8, 8 + rows)
    low = slice(8, 16)
    high = slice(rows, 8 + rows)
    below = slice(0, 8)
    above = slice(8 + rows, 16 + rows)
    left = slice(0, LANES)
    right = slice((blocks - 1) * LANES, blocks * LANES)
    grid_moves = [
        (grid_raw.at[:, low], grid_raw.at[:, above], (0, -1)),
        (grid_raw.at[:, high], grid_raw.at[:, below], (0, 1)),
        (grid_raw.at[:, own, left], grid_side.at[0, :, own], (-1, 0)),
        (grid_raw.at[:, low, left], grid_side.at[0, :, above], (-1, -1)),
        (grid_raw.at[:, high, left], grid_side.at[0, :, below], (-1, 1)),
        (grid_raw.at[:, own, right], grid_side.at[1, :, own], (1, 0)),
        (grid_raw.at[:, low, right], grid_side.at[1, :, above], (1, -1)),
        (grid_raw.at[:, high, right], grid_side.at[1, :, below], (1, 1)),
    ]
    grid_copies = [
        pltpu.make_async_remote_copy(
            src, dst, grid_send_sem.at[i], grid_recv_sem.at[i], device_id=dev(*to), device_id_type=MESH
        )
        for i, (src, dst, to) in enumerate(grid_moves)
    ]
    for copy in grid_copies:
        copy.start()

    def accumulate_own(i, carry):
        acc[i] = term[perm[i]] + acc[prev[i]]
        return carry

    lax.fori_loop(0, capacity, accumulate_own, 0, unroll=4)

    shape = (levels, LANES)
    lane = lax.broadcasted_iota(jnp.int32, shape, 1)
    keep_right = jnp.where(tx < n_tx - 1, 1.0, 0.0).astype(jnp.float32)
    keep_left = jnp.where(tx > 0, 1.0, 0.0).astype(jnp.float32)

    def spread(block, j):
        return jnp.broadcast_to(block[j : j + 1], shape)

    def spread_basis(t, carry):
        at = pl.ds(pl.multiple_of(t * 8, 8), 8)
        for k in range(4):
            for b in range(blocks):
                block = basis_raw[k, at, b * LANES : (b + 1) * LANES]
                for j in range(8):
                    bases[k, t * 8 + j, b] = spread(block, j)
        return carry

    lax.fori_loop(0, rows // 8, spread_basis, 0)

    for copy in grid_copies:
        copy.wait_recv()

    def spread_metric(t, carry, picks=range(8)):
        at = pl.ds(pl.multiple_of(t * 8, 8), 8)
        base = t * 8 - 8 + HALO
        for k in range(3):
            for b in range(blocks):
                block = grid_raw[k, at, b * LANES : (b + 1) * LANES]
                for j in picks:
                    metric[k, base + j, b] = spread(block, j)
            side = jnp.where(lane < LANES // 2, grid_side[0, k, at, :] * keep_right, grid_side[1, k, at, :] * keep_left)
            for j in picks:
                metric[k, base + j, blocks] = spread(side, j)
        return carry

    spread_metric(0, 0, range(8 - HALO, 8))
    lax.fori_loop(1, 1 + rows // 8, spread_metric, 0)
    spread_metric(1 + rows // 8, 0, range(HALO))

    def receive_chunk(c, carry):
        for d in range(1, flows + 1):

            @pl.when(relayed(d))
            def _():
                first_leg(d, c).wait_recv()
                second_leg(d, c).start()

        for d in range(1, flows + 1):
            direct(d, c).wait_recv()
            base = capacity + (c * flows + d - 1) * per

            def add(i, inner):
                acc[base + i] = recv[d - 1, c * per + i] + acc[prev[base + i]]
                return inner

            lax.fori_loop(0, per, add, 0, unroll=6)
        return carry

    lax.fori_loop(0, SEND_CHUNKS, receive_chunk, 0)

    def regrid(r, carry):
        for b in range(blocks):
            patch = acc.at[last[r * blocks + b]]
            east, north, thick = patch[0:levels], patch[levels : 2 * levels], patch[2 * levels : 3 * levels]
            at = pl.ds(r, levels, stride=rows)

            def start(i):
                return state_in.at[i, b].reshape(levels * rows, LANES)[at, :]

            xa[0, r + HALO, b] = start(0) + thick
            xa[1, r + HALO, b] = start(1) + bases[0, r, b] * east + bases[1, r, b] * north
            xa[2, r + HALO, b] = start(2) + bases[2, r, b] * east + bases[3, r, b] * north
        return carry

    lax.fori_loop(0, HALO, regrid, 0)
    lax.fori_loop(rows - HALO, rows, regrid, 0)

    def halo_copy(i, src, dst, to):
        return pltpu.make_async_remote_copy(
            src, dst, halo_send_sem.at[i], halo_recv_sem.at[i], device_id=dev(*to), device_id_type=MESH
        )

    row_copies = [
        halo_copy(0, xa.at[:, HALO : 2 * HALO, 0:blocks], xa.at[:, rows + HALO : rows + 2 * HALO, 0:blocks], (0, -1)),
        halo_copy(1, xa.at[:, rows : rows + HALO, 0:blocks], xa.at[:, 0:HALO, 0:blocks], (0, 1)),
    ]
    for copy in row_copies:
        copy.start()

    lax.fori_loop(HALO, rows - HALO, regrid, 0)

    group = lane // HALO
    packs = packed.shape[1]
    for side in range(2):
        for v in range(packs):
            total = jnp.zeros(shape, jnp.float32)
            for g in range(GROUPS):
                item = v * GROUPS + g
                if item >= 3 * rows:
                    break
                edge = xa[item % 3, item // 3 + HALO, 0 if side == 0 else blocks - 1]
                shift = (HALO * g + (HALO if side else 0)) % LANES
                moved = pltpu.roll(edge, shift, 1) if shift else edge
                total = jnp.where(group == g, moved, total)
            packed[side, v] = total

    strip_copies = []
    for side, dx in ((0, -1), (1, 1)):
        strip_copies += [
            halo_copy(2 + 3 * side, packed.at[side], strips.at[side, 0:packs], (dx, 0)),
            halo_copy(3 + 3 * side, packed.at[side, 0:1], strips.at[side, packs + 1 : packs + 2], (dx, -1)),
            halo_copy(4 + 3 * side, packed.at[side, packs - 1 : packs], strips.at[side, packs : packs + 1], (dx, 1)),
        ]
    for copy in strip_copies:
        copy.start()
    for copy in strip_copies:
        copy.wait_recv()

    for r in range(-HALO, rows + HALO):
        for f in range(3):
            item = 3 * (r % rows) + f
            g = item % GROUPS
            v = item // GROUPS
            if r < 0:
                v = packs
            elif r >= rows:
                v = packs + 1
            from_right = pltpu.roll(strips[0, v], (LANES - HALO * g) % LANES, 1) if g else strips[0, v]
            from_left = pltpu.roll(strips[1, v], (LANES - HALO - HALO * g) % LANES, 1) if g < GROUPS - 1 else strips[1, v]
            xa[f, r + HALO, blocks] = jnp.where(
                lane < HALO,
                from_right * keep_right,
                jnp.where(lane >= LANES - HALO, from_left * keep_left, 0.0),
            )
    for copy in row_copies:
        copy.wait_recv()

    ring = blocks + 1
    is_first = lane == 0
    is_last = lane == LANES - 1
    one = jnp.ones(shape, jnp.float32)
    wall_right = jnp.where(is_last, keep_right, one)
    wall_left = jnp.where(is_last, keep_left, one)

    def from_next(values):
        rolled = [pltpu.roll(v, LANES - 1, 1) for v in values]
        return [jnp.where(is_last, rolled[(b + 1) % ring], rolled[b]) for b in range(ring)]

    def from_before(values):
        rolled = [pltpu.roll(v, 1, 1) for v in values]
        return [jnp.where(is_first, rolled[(b - 1) % ring], rolled[b]) for b in range(ring)]

    def load(src, i):
        depth, con_first, con_second = [], [], []
        for b in range(ring):
            first, second = src[1, i, b], src[2, i, b]
            depth.append(src[0, i, b])
            con_first.append(metric[0, i, b] * first + metric[2, i, b] * second)
            con_second.append(metric[2, i, b] * first + metric[1, i, b] * second)
        return depth, con_first, con_second

    def row_flux(second_low, second_high, depth_low, depth_high):
        out = []
        for b in range(ring):
            face = 0.5 * (second_low[b] + second_high[b])
            out.append(jnp.maximum(face, 0.0) * depth_low[b] + jnp.minimum(face, 0.0) * depth_high[b])
        return out

    def turned(joint, con_first, con_second):
        return [turn[2 * joint] * con_first[b] + turn[2 * joint + 1] * con_second[b] for b in range(ring)]

    def advance_row(src, store, i, carry, joint=None):
        depth_before, (depth, con_first, con_second), flux_below = carry
        after = load(src, i + 1)
        depth_after, first_after, second_after = after
        if joint is None:
            flux_above = row_flux(con_second, second_after, depth, depth_after)
            flux_next = flux_above
        else:
            flux_above = row_flux(con_second, turned(joint, first_after, second_after), depth, depth_after)
            flux_next = row_flux(turned(joint + 1, con_first, con_second), second_after, depth, depth_after)
        depth_right = from_next(depth)
        first_right = from_next(con_first)
        flux_right = []
        for b in range(ring):
            face = 0.5 * (con_first[b] + first_right[b])
            if b == blocks - 1:
                face = face * wall_right
            if b == blocks:
                face = face * wall_left
            flux_right.append(jnp.maximum(face, 0.0) * depth[b] + jnp.minimum(face, 0.0) * depth_right[b])
        depth_left = from_before(depth)
        flux_left = from_before(flux_right)
        for b in range(ring):
            new_depth = depth[b] - COURANT * ((flux_right[b] - flux_left[b]) + (flux_above[b] - flux_below[b]))
            new_first = src[1, i, b] - HALF_GRADIENT * (depth_right[b] - depth_left[b])
            new_second = src[2, i, b] - HALF_GRADIENT * (depth_after[b] - depth_before[b])
            store(i, b, (new_depth, new_first, new_second))
        return (depth, after, flux_next)

    for step in range(STEPS):
        src, dst = (xa, xb) if step % 2 == 0 else (xb, xa)
        margin = STEPS - 1 - step

        def store_state(i, b, values, dst=dst):
            for f in range(3):
                dst[f, i, b] = values[f]

        def store_out(i, b, values):
            if b < blocks:
                for f in range(3):
                    out_v.at[f, b].reshape(levels * rows, LANES)[pl.ds(i - HALO, levels, stride=rows), :] = values[f]

        if step == 1:
            for copy in row_copies:
                copy.wait_send()
        store = store_out if step == STEPS - 1 else store_state
        start = HALO - margin
        before, current = load(src, start - 1), load(src, start)
        if margin == 0:
            flux = row_flux(turned(1, before[1], before[2]), current[2], before[0], current[0])
        else:
            flux = row_flux(before[2], current[2], before[0], current[0])
        carry = (before[0], current, flux)
        for i in range(start, HALO):
            carry = advance_row(src, store, i, carry, 0 if i == HALO - 1 else None)
        carry = lax.fori_loop(
            HALO, HALO + rows - 1, lambda i, c, src=src, store=store: advance_row(src, store, i, c), carry
        )
        carry = advance_row(src, store, HALO + rows - 1, carry, 2)
        for i in range(HALO + rows, HALO + rows + margin):
            carry = advance_row(src, store, i, carry)

    out_copies = [
        pltpu.make_async_copy(out_v.at[f, b], out.at[:, :, b * LANES : (b + 1) * LANES], out_sem.at[f, b])
        for f, out in enumerate((out_depth, out_first, out_second))
        for b in range(blocks)
    ]
    for copy in out_copies:
        copy.start()
    for d in range(1, flows + 1):

        def sent(c, carry):
            direct(d, c).wait_send()

            @pl.when(relayed(d))
            def _():
                second_leg(d, c).wait_send()

            return carry

        lax.fori_loop(0, SEND_CHUNKS, sent, 0)
    for copy in grid_copies + strip_copies:
        copy.wait_send()
    for copy in out_copies:
        copy.wait()


def body(
    increments, remap_weights, dest_offset, slot_patch, rotation, basis,
    inv_metric_diag, inv_metric_cross, thickness, wind_first, wind_second,
):
    levels, rows, cols = thickness.shape
    lat_rows, top, patch, cells = remap_weights.shape[2:]
    pairs = 3 * levels
    entries = lat_rows * top
    owners, capacity = slot_patch.shape[2:]
    flows = owners - 1
    slots = owners * capacity
    blocks = cols // LANES
    patches = rows * blocks
    per = capacity // SEND_CHUNKS
    ty = lax.axis_index("ty")

    offsets = dest_offset.reshape(entries)
    ids = jnp.arange(entries, dtype=jnp.int32)
    same = (offsets[:, None] == offsets[None, :]) & (ids[None, :] < ids[:, None])
    position = offsets * capacity + jnp.sum(same.astype(jnp.int32), axis=1)
    slot_ids = jnp.arange(slots, dtype=jnp.int32)
    perm = jnp.min(jnp.where(position[None, :] == slot_ids[:, None], ids[None, :], entries), axis=1)
    table = slot_patch[0, 0]
    arrivals = table[1:].reshape(flows, SEND_CHUNKS, per).transpose(1, 0, 2).reshape(-1)
    order = jnp.concatenate([table[0], arrivals])
    match = (order[:, None] == order[None, :]) & (slot_ids[None, :] < slot_ids[:, None])
    prev = jnp.max(jnp.where(match, slot_ids[None, :], -1), axis=1)
    prev = jnp.where(prev < 0, slots, prev)
    patch_ids = jnp.arange(patches, dtype=jnp.int32)
    last = jnp.max(jnp.where(order[None, :] == patch_ids[:, None], slot_ids[None, :], -1), axis=1)
    last = jnp.where(last < 0, slots, last)

    tiles = lax.axis_size("ty") // PANELS
    panel = ty // tiles
    at_low = ty % tiles == 0
    at_high = ty % tiles == tiles - 1
    codes = jnp.stack(
        [
            jnp.where(at_low, rotation[1, (panel + PANELS - 1) % PANELS], 0),
            jnp.where(at_low, rotation[0, panel], 0),
            jnp.where(at_high, rotation[1, panel], 0),
            jnp.where(at_high, rotation[0, (panel + 1) % PANELS], 0),
        ]
    )
    cosine = (codes == 0).astype(jnp.float32) - (codes == 2).astype(jnp.float32)
    sine = (codes == 1).astype(jnp.float32) - (codes == 3).astype(jnp.float32)
    turn = jnp.stack([sine, cosine], axis=1).reshape(-1)

    f32 = jnp.float32
    hrows = rows + 2 * HALO
    packs = -(-3 * rows // GROUPS)
    vmem, dma = pltpu.VMEM, pltpu.SemaphoreType.DMA
    scratch = [
        vmem((W_SLOTS, W_ROWS, top * patch, cells), jnp.bfloat16),
        vmem((pairs, lat_rows, cells), jnp.bfloat16),
        vmem((pairs * W_ROWS, LANES), f32),
        vmem((pairs * W_ROWS, LANES), f32),
        vmem((entries + 1, pairs, LANES), f32),
        vmem((flows, capacity, pairs, LANES), f32),
        vmem((flows, capacity, pairs, LANES), f32),
        vmem((flows, capacity, pairs, LANES), f32),
        vmem((slots + 1, pairs, LANES), f32),
        vmem((3, hrows, blocks + 1, levels, LANES), f32),
        vmem((3, hrows, blocks + 1, levels, LANES), f32),
        vmem((3, hrows, blocks + 1, levels, LANES), f32),
        vmem((4, rows, blocks, levels, LANES), f32),
        vmem((3, blocks, levels, rows, LANES), f32),
        vmem((3, blocks, levels, rows, LANES), f32),
        vmem((3, rows + 16, cols), f32),
        vmem((2, 3, rows + 16, LANES), f32),
        vmem((4, rows, cols), f32),
        vmem((2, packs, levels, LANES), f32),
        vmem((2, packs + 2, levels, LANES), f32),
        dma((W_SLOTS,)),
        dma,
        dma((3 + 3 * blocks,)),
        dma((3, blocks)),
        dma((flows, SEND_CHUNKS)),
        dma((flows, SEND_CHUNKS)),
        dma((flows, SEND_CHUNKS)),
        dma((flows, SEND_CHUNKS)),
        dma((8,)),
        dma((8,)),
        dma((8,)),
        dma((8,)),
    ]
    anywhere = pl.BlockSpec(memory_space=pl.ANY)
    scalars = pl.BlockSpec(memory_space=pltpu.SMEM)
    return pl.pallas_call(
        kernel,
        out_shape=[jax.ShapeDtypeStruct(thickness.shape, f32)] * 3,
        in_specs=[scalars] * 4 + [anywhere] * 8,
        out_specs=[anywhere] * 3,
        scratch_shapes=scratch,
        compiler_params=pltpu.CompilerParams(
            collective_id=0, has_side_effects=True, vmem_limit_bytes=62 * 1024 * 1024
        ),
    )(
        perm, prev, last, turn,
        increments.reshape(pairs, lat_rows, cells),
        remap_weights.reshape(lat_rows, top * patch, cells),
        basis, inv_metric_diag, inv_metric_cross, thickness, wind_first, wind_second,
    )


def solution(mesh):
    tile = P(None, "ty", "tx")
    in_specs = (
        P(None, None, "tx", "ty"),
        P("tx", "ty", None, None, None, None),
        P("tx", "ty", None, None),
        P("tx", "ty", None, None),
        P(),
        tile,
        tile,
        P("ty", "tx"),
        tile,
        tile,
        tile,
    )
    return jax.shard_map(body, mesh=mesh, in_specs=in_specs, out_specs=(tile, tile, tile), check_vma=False)
```

time: 222 us -> 163 us (0.73)
  Pallas kernels: 0 us -> 144 us
  waiting for transfers between devices: 107 us -> 0 us
  starting transfers between devices: 45.2 us -> 0 us
  other arithmetic: 31.9 us -> 2.71 us
  local copies, waits for them, and re-layouts: 26 us -> 10.4 us
  matrix products: 10.7 us -> 0 us
  between operations: 1.11 us -> 3.37 us
    pallas_call x0 -> x1, Pallas kernels: none -> 144 us  [body(): pl.pallas_call(kernel, out_shape=[jax.ShapeDtypeStruct(thickness.shape, f...]
    ppermute x19 -> x0, waiting for transfers between devices: 107 us -> none  [the longest x3 88.5 us: from_behind(): lax.ppermute(array, axis, [(i, (i + by) % size) for i in range(size)])]
    ppermute x19 -> x0, starting transfers between devices: 45.2 us -> none  [the longest x8 20.9 us: padded(): lax.ppermute(tail, axis, [(i, (i + 1) % count) for i in range(ends)])]
    dot_general x1 -> x0, matrix products: 10.7 us -> none  [body(): jnp.einsum('clsk,stpk->stclp', increments, remap_weights[0, 0], preferred...]
    another operation x12 -> x1, other arithmetic: 9.9 us -> 0.01 us  [body(): turn = jnp.stack([sine, cosine], axis=1).reshape(-1)]
    scatter-add x1 -> x0, other arithmetic: 9.81 us -> none  [body(): patches = jnp.zeros((patch_count, row_width), jnp.float32).at[slot_patch....]
    sub x6 -> x2, other arithmetic: 9.16 us -> 0.08 us  [the longest x1 0.08 us: body(): sine = (codes == 1).astype(jnp.float32) - (codes == 3).astype(jnp.float32)]
    reshape x3 -> x5, local copies, waits for them, and re-layouts: 9.32 us -> 0.95 us  [the longest x1 0.62 us: body(): turn = jnp.stack([sine, cosine], axis=1).reshape(-1)]
  transfers between devices with their start and end apart: 19 -> 0, of which waited for: 10 -> 0; matrix products, arithmetic and copies ran while one was open for 1% -> 0% of each run, Pallas kernels for 0% -> 0%
where the time goes in v1:
time: 163 us; the launch traced here: 161 us
  Pallas kernels  144 us (88%)
  local copies, waits for them, and re-layouts  10.4 us (6%)
  between operations  3.37 us (2%)
  other arithmetic  2.71 us (2%)
    pallas_call x1, Pallas kernels, body(): pl.pallas_call(kernel, out_shape=[jax.ShapeDtypeStruct(thickness.shape, f...  144 us
    unnamed x4, local copies, waits for them, and re-layouts  6.53 us

profile of v1, /device:TPU:1, one launch (start us, length us, event | category | flops | bytes accessed | tf_op | source)
XLA Modules:
  0.0 160.9 jit_solution(1921071578883937391)
XLA Ops:
  0.7 0.7 slice_bitcast_fusion
  1.4 1.5 constant_dynamic-slice_fusion.1
  5.5 0.1 fusion.2
  5.6 0.1 copy.21
  5.7 0.6 reshape.281.turn
  6.3 0.7 slice.9
  7.0 0.1 reshape.279
  7.1 0.1 reshape.280
  7.2 0.1 pad_add_fusion
  7.3 0.1 select_reduce_fusion.2
  7.4 0.3 select_reduce_fusion
  7.7 0.6 compare_select_fusion.prev
  8.3 0.6 compare_select_fusion.1.last
  8.9 0.8 copy.19
  9.6 0.1 reshape.278
  9.8 0.2 convert_reduce_fusion
  10.0 0.8 select_reduce_fusion.1.perm
  10.8 144.4 %shard_map.130 = (f32[8,48,384]{2,1,0:T(8,128)}, f32[8,48,384]{2,1,0:T(8,128)}, f32[8,48,384]{2,1,0:T(8,128)}) custom-call(s32[432]{0:T(512)} %select_reduce_fusion.1.perm, s32[432]{0:T(512)} %compare_select_fusion.prev, s32[144]{0:T(256)} %compare_select_fusion.1.last, f32[8]{0:T(128)} %reshape.281.turn, bf16[24,144,256]{2,1,0:T(8,128)(2,1)} %bitcast.18, ...), custom_call_target="tpu_custom_call" | custom-call | tf_op jit(solution)/shard_map/pallas_call | solution.py:538
  155.1 1.9 %copy.27 = f32[8,48,384]{2,1,0:T(8,128)} copy(f32[8,48,384]{2,1,0:T(8,128)} %get-tuple-element.12) | data formatting | bytes 1179648
  157.0 1.9 %copy.28 = f32[8,48,384]{2,1,0:T(8,128)} copy(f32[8,48,384]{2,1,0:T(8,128)} %get-tuple-element.13) | data formatting | bytes 1179648
  159.0 1.9 %copy.29 = f32[8,48,384]{2,1,0:T(8,128)} copy(f32[8,48,384]{2,1,0:T(8,128)} %get-tuple-element.14) | data formatting | bytes 1179648
  (4 shorter events, 0.0 us)

commit v2 on v1

--- a/solution.py
+++ b/solution.py
@@ -15,16 +15,19 @@
 GROUPS = 32
 NX = 4
 SEND_CHUNKS = 6
+LAG = 1
+EDGE = HALO + 1
+ROWS = 4
 W_SLOTS = 4
 W_ROWS = 16
 
 
 def kernel(
-    perm, prev, last, turn, inc, wts, basis, diag, cross, depth_in, first_in, second_in,
+    offsets, patches, rotation, inc, wts, basis, diag, cross, depth_in, first_in, second_in,
     out_depth, out_first, out_second,
     wbuf, inc_v, half0, half1, term, send, recv, relay, acc, xa, xb, metric, bases,
-    state_in, out_v, grid_raw, grid_side, basis_raw, packed, strips,
-    w_sem, in_sem, field_sem, out_sem, send_sem, recv_sem, relay_send_sem, relay_recv_sem,
+    state_in, out_v, grid_raw, grid_side, basis_raw, packed, strips, off_v, patch_v, table_v, table,
+    w_sem, in_sem, table_sem, field_sem, out_sem, send_sem, recv_sem, relay_send_sem, relay_recv_sem,
     grid_send_sem, grid_recv_sem, halo_send_sem, halo_recv_sem,
 ):
     tx = lax.axis_index("tx")
@@ -73,6 +76,68 @@
     for copy in field_copies:
         copy.start()
 
+    owners = flows + 1
+    square = (LANES, LANES)
+    row_id = lax.broadcasted_iota(jnp.int32, square, 0)
+    col_id = lax.broadcasted_iota(jnp.int32, square, 1)
+    tops, lat_rows = offsets.shape
+    off_v[...] = jnp.full(off_v.shape, owners, jnp.int32)
+    off_v[0:tops, 0:lat_rows] = offsets[...]
+    patch_v[...] = jnp.full(patch_v.shape, -1, jnp.int32)
+    patch_v[0:owners, 0:capacity] = patches[...]
+    off = [off_v[t : t + 1, :] for t in range(tops)]
+    wide = off_v.shape[1]
+    hits = [[(off[t] == d).astype(jnp.float32) for t in range(tops)] for d in range(owners)]
+    stacked = jnp.concatenate([jnp.broadcast_to(hits[d][t], (8, wide)) for d in range(owners) for t in range(tops)], axis=0)
+    before_mask = lax.broadcasted_iota(jnp.int32, (wide, wide), 0) < lax.broadcasted_iota(jnp.int32, (wide, wide), 1)
+    counts = jnp.dot(
+        stacked.astype(jnp.bfloat16), before_mask.astype(jnp.bfloat16), preferred_element_type=jnp.float32
+    )
+    place = []
+    for t in range(tops):
+        rank = jnp.zeros((1, wide), jnp.float32)
+        for d in range(owners):
+            earlier = sum(counts[8 * (d * tops + u) : 8 * (d * tops + u) + 1] for u in range(tops))
+            earlier = earlier + sum(hits[d][u] for u in range(t)) if t else earlier
+            rank = rank + hits[d][t] * earlier
+        place.append(off[t] * LANES + rank.astype(jnp.int32))
+    found = [jnp.zeros((1, LANES), jnp.int32) for _ in range(owners)]
+    for t in range(tops):
+        for h in range(wide // LANES):
+            column = jnp.transpose(jnp.broadcast_to(place[t][:, h * LANES : (h + 1) * LANES], square))
+            entry = (row_id + h * LANES) * tops + t - entries
+            for d in range(owners):
+                hit = jnp.where(column == col_id + d * LANES, entry, 0)
+                found[d] = found[d] + jnp.sum(hit, axis=0, keepdims=True)
+    for d in range(owners):
+        table_v[d : d + 1, :] = found[d] + entries
+
+    def order(d, k):
+        if d == 0:
+            return jnp.where(k < capacity, k, slots)
+        chunk = k // per
+        return jnp.where(k < capacity, capacity + (chunk * flows + d - 1) * per + (k - chunk * per), slots)
+
+    column_patch = [jnp.transpose(jnp.broadcast_to(patch_v[d : d + 1, :], square)) for d in range(owners)]
+    column_order = [order(d, row_id) for d in range(owners)]
+    for d in range(owners):
+        mine, target = patch_v[d : d + 1, :], order(d, col_id)
+        best = jnp.full(square, -1, jnp.int32)
+        for e in range(owners):
+            hit = jnp.logical_and(column_patch[e] == mine, column_order[e] < target)
+            best = jnp.maximum(best, jnp.where(hit, column_order[e], -1))
+        best = jnp.max(best, axis=0, keepdims=True)
+        table_v[owners + d : owners + d + 1, :] = jnp.where(best < 0, slots, best)
+    for h in range(2):
+        best = jnp.full(square, -1, jnp.int32)
+        for e in range(owners):
+            hit = jnp.logical_and(column_patch[e] == col_id + h * LANES, column_order[e] < slots)
+            best = jnp.maximum(best, jnp.where(hit, column_order[e], -1))
+        best = jnp.max(best, axis=0, keepdims=True)
+        table_v[2 * owners + h : 2 * owners + h + 1, :] = jnp.where(best < 0, slots, best)
+    table_copy = pltpu.make_async_copy(table_v, table, table_sem)
+    table_copy.start()
+
     zero_row = jnp.zeros(term.shape[1:], jnp.float32)
     term[entries] = zero_row
     acc[slots] = zero_row
@@ -106,6 +171,7 @@
 
     lax.fori_loop(0, w_chunks, term_chunk, 0)
 
+    table_copy.wait()
     pl.semaphore_wait(barrier, len(partners))
 
     def direct(d, c):
@@ -132,12 +198,20 @@
     def relayed(d):
         return jnp.logical_and(odd, x + d >= NX)
 
+    def forward(c):
+        for d in range(1, flows + 1):
+
+            @pl.when(relayed(d))
+            def _():
+                first_leg(d, c).wait_recv()
+                second_leg(d, c).start()
+
     def send_chunk(c, carry):
         for d in range(1, flows + 1):
 
             def gather(i, inner):
                 k = c * per + i
-                send[d - 1, k] = term[perm[d * capacity + k]]
+                send[d - 1, k] = term[table[d, k]]
                 return inner
 
             lax.fori_loop(0, per, gather, 0, unroll=6)
@@ -150,9 +224,15 @@
             def _():
                 direct(d, c).start()
 
+        @pl.when(c >= LAG)
+        def _():
+            forward(c - LAG)
+
         return carry
 
     lax.fori_loop(0, SEND_CHUNKS, send_chunk, 0)
+    for c in range(SEND_CHUNKS - LAG, SEND_CHUNKS):
+        forward(c)
 
     for copy in field_copies:
         copy.wait()
@@ -184,7 +264,7 @@
         copy.start()
 
     def accumulate_own(i, carry):
-        acc[i] = term[perm[i]] + acc[prev[i]]
+        acc[i] = term[table[0, i]] + acc[table[owners, i]]
         return carry
 
     lax.fori_loop(0, capacity, accumulate_own, 0, unroll=4)
@@ -213,7 +293,7 @@
 
     def spread_metric(t, carry, picks=range(8)):
         at = pl.ds(pl.multiple_of(t * 8, 8), 8)
-        base = t * 8 - 8 + HALO
+        base = t * 8 - 8 + EDGE
         for k in range(3):
             for b in range(blocks):
                 block = grid_raw[k, at, b * LANES : (b + 1) * LANES]
@@ -230,18 +310,11 @@
 
     def receive_chunk(c, carry):
         for d in range(1, flows + 1):
-
-            @pl.when(relayed(d))
-            def _():
-                first_leg(d, c).wait_recv()
-                second_leg(d, c).start()
-
-        for d in range(1, flows + 1):
             direct(d, c).wait_recv()
             base = capacity + (c * flows + d - 1) * per
 
             def add(i, inner):
-                acc[base + i] = recv[d - 1, c * per + i] + acc[prev[base + i]]
+                acc[base + i] = recv[d - 1, c * per + i] + acc[table[owners + d, c * per + i]]
                 return inner
 
             lax.fori_loop(0, per, add, 0, unroll=6)
@@ -251,16 +324,17 @@
 
     def regrid(r, carry):
         for b in range(blocks):
-            patch = acc.at[last[r * blocks + b]]
+            q = r * blocks + b
+            patch = acc.at[table[2 * owners + q // LANES, lax.rem(q, LANES)]]
             east, north, thick = patch[0:levels], patch[levels : 2 * levels], patch[2 * levels : 3 * levels]
             at = pl.ds(r, levels, stride=rows)
 
             def start(i):
                 return state_in.at[i, b].reshape(levels * rows, LANES)[at, :]
 
-            xa[0, r + HALO, b] = start(0) + thick
-            xa[1, r + HALO, b] = start(1) + bases[0, r, b] * east + bases[1, r, b] * north
-            xa[2, r + HALO, b] = start(2) + bases[2, r, b] * east + bases[3, r, b] * north
+            xa[0, r + EDGE, b] = start(0) + thick
+            xa[1, r + EDGE, b] = start(1) + bases[0, r, b] * east + bases[1, r, b] * north
+            xa[2, r + EDGE, b] = start(2) + bases[2, r, b] * east + bases[3, r, b] * north
         return carry
 
     lax.fori_loop(0, HALO, regrid, 0)
@@ -272,8 +346,8 @@
         )
 
     row_copies = [
-        halo_copy(0, xa.at[:, HALO : 2 * HALO, 0:blocks], xa.at[:, rows + HALO : rows + 2 * HALO, 0:blocks], (0, -1)),
-        halo_copy(1, xa.at[:, rows : rows + HALO, 0:blocks], xa.at[:, 0:HALO, 0:blocks], (0, 1)),
+        halo_copy(0, xa.at[:, EDGE : EDGE + HALO, 0:blocks], xa.at[:, EDGE + rows : EDGE + rows + HALO, 0:blocks], (0, -1)),
+        halo_copy(1, xa.at[:, EDGE + rows - HALO : EDGE + rows, 0:blocks], xa.at[:, EDGE - HALO : EDGE, 0:blocks], (0, 1)),
     ]
     for copy in row_copies:
         copy.start()
@@ -289,7 +363,7 @@
                 item = v * GROUPS + g
                 if item >= 3 * rows:
                     break
-                edge = xa[item % 3, item // 3 + HALO, 0 if side == 0 else blocks - 1]
+                edge = xa[item % 3, item // 3 + EDGE, 0 if side == 0 else blocks - 1]
                 shift = (HALO * g + (HALO if side else 0)) % LANES
                 moved = pltpu.roll(edge, shift, 1) if shift else edge
                 total = jnp.where(group == g, moved, total)
@@ -318,20 +392,19 @@
                 v = packs + 1
             from_right = pltpu.roll(strips[0, v], (LANES - HALO * g) % LANES, 1) if g else strips[0, v]
             from_left = pltpu.roll(strips[1, v], (LANES - HALO - HALO * g) % LANES, 1) if g < GROUPS - 1 else strips[1, v]
-            xa[f, r + HALO, blocks] = jnp.where(
+            xa[f, r + EDGE, blocks] = jnp.where(
                 lane < HALO,
                 from_right * keep_right,
                 jnp.where(lane >= LANES - HALO, from_left * keep_left, 0.0),
             )
-    for copy in row_copies:
-        copy.wait_recv()
-
     ring = blocks + 1
     is_first = lane == 0
     is_last = lane == LANES - 1
     one = jnp.ones(shape, jnp.float32)
     wall_right = jnp.where(is_last, keep_right, one)
     wall_left = jnp.where(is_last, keep_left, one)
+    wall_right_halo = jnp.where(is_first, keep_right, one)
+    wall_left_tile = jnp.where(is_first, keep_left, one)
 
     def from_next(values):
         rolled = [pltpu.roll(v, LANES - 1, 1) for v in values]
@@ -357,41 +430,79 @@
             out.append(jnp.maximum(face, 0.0) * depth_low[b] + jnp.minimum(face, 0.0) * depth_high[b])
         return out
 
-    def turned(joint, con_first, con_second):
-        return [turn[2 * joint] * con_first[b] + turn[2 * joint + 1] * con_second[b] for b in range(ring)]
-
-    def advance_row(src, store, i, carry, joint=None):
-        depth_before, (depth, con_first, con_second), flux_below = carry
-        after = load(src, i + 1)
-        depth_after, first_after, second_after = after
-        if joint is None:
-            flux_above = row_flux(con_second, second_after, depth, depth_after)
-            flux_next = flux_above
-        else:
-            flux_above = row_flux(con_second, turned(joint, first_after, second_after), depth, depth_after)
-            flux_next = row_flux(turned(joint + 1, con_first, con_second), second_after, depth, depth_after)
-        depth_right = from_next(depth)
-        first_right = from_next(con_first)
-        flux_right = []
-        for b in range(ring):
-            face = 0.5 * (con_first[b] + first_right[b])
-            if b == blocks - 1:
-                face = face * wall_right
-            if b == blocks:
-                face = face * wall_left
-            flux_right.append(jnp.maximum(face, 0.0) * depth[b] + jnp.minimum(face, 0.0) * depth_right[b])
-        depth_left = from_before(depth)
-        flux_left = from_before(flux_right)
-        for b in range(ring):
-            new_depth = depth[b] - COURANT * ((flux_right[b] - flux_left[b]) + (flux_above[b] - flux_below[b]))
-            new_first = src[1, i, b] - HALF_GRADIENT * (depth_right[b] - depth_left[b])
-            new_second = src[2, i, b] - HALF_GRADIENT * (depth_after[b] - depth_before[b])
-            store(i, b, (new_depth, new_first, new_second))
-        return (depth, after, flux_next)
+    tiles = n_ty // PANELS
+    panel = ty // tiles
+    place_in_panel = lax.rem(ty, tiles)
+
+    def joint(present, code):
+        code = jnp.where(present, code, 0)
+
+        def equals(value):
+            return jnp.where(code == value, 1.0, 0.0).astype(jnp.float32)
+
+        return equals(1) - equals(3), equals(0) - equals(2)
+
+    low_joint, high_joint = place_in_panel == 0, place_in_panel == tiles - 1
+    low_above = joint(low_joint, rotation[1, lax.rem(panel + PANELS - 1, PANELS)])
+    low_below = joint(low_joint, rotation[0, panel])
+    high_above = joint(high_joint, rotation[1, panel])
+    high_below = joint(high_joint, rotation[0, lax.rem(panel + 1, PANELS)])
+    groups = rows // ROWS
+
+    def pick(group, low_turn, high_turn):
+        return [
+            jnp.where(group == 0, low_turn[k], jnp.where(group == groups, high_turn[k], float(k))) for k in range(2)
+        ]
+
+    def turned(turn, con_first, con_second):
+        return [turn[0] * con_first[b] + turn[1] * con_second[b] for b in range(ring)]
+
+    def flux_into(src, group):
+        i = EDGE - ROWS + group * ROWS
+        low, high = load(src, i - 1), load(src, i)
+        turn = pick(group - 1, low_below, high_below)
+        return row_flux(turned(turn, low[1], low[2]), high[2], low[0], high[0])
+
+    def advance_group(src, store, group, flux_below):
+        i = EDGE - ROWS + group * ROWS
+        depth_before = [src[0, i - 1, b] for b in range(ring)]
+        current = load(src, i)
+        for j in range(ROWS):
+            depth, con_first, con_second = current
+            after = load(src, i + j + 1)
+            depth_after, first_after, second_after = after
+            if j < ROWS - 1:
+                flux_above = row_flux(con_second, second_after, depth, depth_after)
+                flux_next = flux_above
+            else:
+                turn_above = pick(group, low_above, high_above)
+                turn_below = pick(group, low_below, high_below)
+                flux_above = row_flux(con_second, turned(turn_above, first_after, second_after), depth, depth_after)
+                flux_next = row_flux(turned(turn_below, con_first, con_second), second_after, depth, depth_after)
+            depth_right, first_right = from_next(depth), from_next(con_first)
+            depth_left, first_left = from_before(depth), from_before(con_first)
+            for b in range(ring):
+                face = 0.5 * (con_first[b] + first_right[b])
+                if b == blocks - 1:
+                    face = face * wall_right
+                if b == blocks:
+                    face = face * wall_left
+                flux_right = jnp.maximum(face, 0.0) * depth[b] + jnp.minimum(face, 0.0) * depth_right[b]
+                face = 0.5 * (con_first[b] + first_left[b])
+                if b == blocks:
+                    face = face * wall_right_halo
+                if b == 0:
+                    face = face * wall_left_tile
+                flux_left = jnp.maximum(face, 0.0) * depth_left[b] + jnp.minimum(face, 0.0) * depth[b]
+                new_depth = depth[b] - COURANT * ((flux_right - flux_left) + (flux_above[b] - flux_below[b]))
+                new_first = src[1, i + j, b] - HALF_GRADIENT * (depth_right[b] - depth_left[b])
+                new_second = src[2, i + j, b] - HALF_GRADIENT * (depth_after[b] - depth_before[b])
+                store(i + j, b, (new_depth, new_first, new_second))
+            depth_before, current, flux_below = depth, after, flux_next
+        return flux_below
 
     for step in range(STEPS):
         src, dst = (xa, xb) if step % 2 == 0 else (xb, xa)
-        margin = STEPS - 1 - step
 
         def store_state(i, b, values, dst=dst):
             for f in range(3):
@@ -400,27 +511,27 @@
         def store_out(i, b, values):
             if b < blocks:
                 for f in range(3):
-                    out_v.at[f, b].reshape(levels * rows, LANES)[pl.ds(i - HALO, levels, stride=rows), :] = values[f]
-
-        if step == 1:
+                    out_v.at[f, b].reshape(levels * rows, LANES)[pl.ds(i - EDGE, levels, stride=rows), :] = values[f]
+
+        store = store_out if step == STEPS - 1 else store_state
+
+        def sweep(first, end, src=src, store=store):
+            lax.fori_loop(
+                first, end, lambda g, flux: tuple(advance_group(src, store, g, flux)), tuple(flux_into(src, first))
+            )
+
+        if step == 0:
+            sweep(2, groups)
+            for copy in row_copies:
+                copy.wait_recv()
+            sweep(0, 2)
+            sweep(groups, groups + 2)
             for copy in row_copies:
                 copy.wait_send()
-        store = store_out if step == STEPS - 1 else store_state
-        start = HALO - margin
-        before, current = load(src, start - 1), load(src, start)
-        if margin == 0:
-            flux = row_flux(turned(1, before[1], before[2]), current[2], before[0], current[0])
+        elif step < STEPS - 1:
+            sweep(0, groups + 2)
         else:
-            flux = row_flux(before[2], current[2], before[0], current[0])
-        carry = (before[0], current, flux)
-        for i in range(start, HALO):
-            carry = advance_row(src, store, i, carry, 0 if i == HALO - 1 else None)
-        carry = lax.fori_loop(
-            HALO, HALO + rows - 1, lambda i, c, src=src, store=store: advance_row(src, store, i, c), carry
-        )
-        carry = advance_row(src, store, HALO + rows - 1, carry, 2)
-        for i in range(HALO + rows, HALO + rows + margin):
-            carry = advance_row(src, store, i, carry)
+            sweep(1, groups + 1)
 
     out_copies = [
         pltpu.make_async_copy(out_v.at[f, b], out.at[:, :, b * LANES : (b + 1) * LANES], out_sem.at[f, b])
@@ -459,44 +570,8 @@
     flows = owners - 1
     slots = owners * capacity
     blocks = cols // LANES
-    patches = rows * blocks
-    per = capacity // SEND_CHUNKS
-    ty = lax.axis_index("ty")
-
-    offsets = dest_offset.reshape(entries)
-    ids = jnp.arange(entries, dtype=jnp.int32)
-    same = (offsets[:, None] == offsets[None, :]) & (ids[None, :] < ids[:, None])
-    position = offsets * capacity + jnp.sum(same.astype(jnp.int32), axis=1)
-    slot_ids = jnp.arange(slots, dtype=jnp.int32)
-    perm = jnp.min(jnp.where(position[None, :] == slot_ids[:, None], ids[None, :], entries), axis=1)
-    table = slot_patch[0, 0]
-    arrivals = table[1:].reshape(flows, SEND_CHUNKS, per).transpose(1, 0, 2).reshape(-1)
-    order = jnp.concatenate([table[0], arrivals])
-    match = (order[:, None] == order[None, :]) & (slot_ids[None, :] < slot_ids[:, None])
-    prev = jnp.max(jnp.where(match, slot_ids[None, :], -1), axis=1)
-    prev = jnp.where(prev < 0, slots, prev)
-    patch_ids = jnp.arange(patches, dtype=jnp.int32)
-    last = jnp.max(jnp.where(order[None, :] == patch_ids[:, None], slot_ids[None, :], -1), axis=1)
-    last = jnp.where(last < 0, slots, last)
-
-    tiles = lax.axis_size("ty") // PANELS
-    panel = ty // tiles
-    at_low = ty % tiles == 0
-    at_high = ty % tiles == tiles - 1
-    codes = jnp.stack(
-        [
-            jnp.where(at_low, rotation[1, (panel + PANELS - 1) % PANELS], 0),
-            jnp.where(at_low, rotation[0, panel], 0),
-            jnp.where(at_high, rotation[1, panel], 0),
-            jnp.where(at_high, rotation[0, (panel + 1) % PANELS], 0),
-        ]
-    )
-    cosine = (codes == 0).astype(jnp.float32) - (codes == 2).astype(jnp.float32)
-    sine = (codes == 1).astype(jnp.float32) - (codes == 3).astype(jnp.float32)
-    turn = jnp.stack([sine, cosine], axis=1).reshape(-1)
-
     f32 = jnp.float32
-    hrows = rows + 2 * HALO
+    hrows = rows + 2 * EDGE
     packs = -(-3 * rows // GROUPS)
     vmem, dma = pltpu.VMEM, pltpu.SemaphoreType.DMA
     scratch = [
@@ -520,7 +595,12 @@
         vmem((4, rows, cols), f32),
         vmem((2, packs, levels, LANES), f32),
         vmem((2, packs + 2, levels, LANES), f32),
+        vmem((8, 2 * LANES), jnp.int32),
+        vmem((8, LANES), jnp.int32),
+        vmem((16, LANES), jnp.int32),
+        pltpu.SMEM((16, LANES), jnp.int32),
         dma((W_SLOTS,)),
+        dma,
         dma,
         dma((3 + 3 * blocks,)),
         dma((3, blocks)),
@@ -534,22 +614,38 @@
         dma((8,)),
     ]
     anywhere = pl.BlockSpec(memory_space=pl.ANY)
-    scalars = pl.BlockSpec(memory_space=pltpu.SMEM)
-    return pl.pallas_call(
+    on_chip = pl.BlockSpec(memory_space=pltpu.VMEM)
+    moved = pl.pallas_call(
         kernel,
         out_shape=[jax.ShapeDtypeStruct(thickness.shape, f32)] * 3,
-        in_specs=[scalars] * 4 + [anywhere] * 8,
+        in_specs=[on_chip, on_chip, pl.BlockSpec(memory_space=pltpu.SMEM)] + [anywhere] * 8,
         out_specs=[anywhere] * 3,
         scratch_shapes=scratch,
         compiler_params=pltpu.CompilerParams(
             collective_id=0, has_side_effects=True, vmem_limit_bytes=62 * 1024 * 1024
         ),
     )(
-        perm, prev, last, turn,
+        dest_offset[0, 0].T, slot_patch[0, 0], rotation,
         increments.reshape(pairs, lat_rows, cells),
         remap_weights.reshape(lat_rows, top * patch, cells),
         basis, inv_metric_diag, inv_metric_cross, thickness, wind_first, wind_second,
     )
+    spec = pl.BlockSpec((levels // 4, rows, cols), lambda i: (i, 0, 0))
+    return tuple(
+        pl.pallas_call(
+            copy_kernel,
+            out_shape=[jax.ShapeDtypeStruct(thickness.shape, f32)] * 3,
+            grid=(4,),
+            in_specs=[spec] * 3,
+            out_specs=[spec] * 3,
+        )(*moved)
+    )
+
+
+def copy_kernel(depth, first, second, out_depth, out_first, out_second):
+    out_depth[...] = depth[...]
+    out_first[...] = first[...]
+    out_second[...] = second[...]
 
 
 def solution(mesh):

time: 163 us -> 102 us (0.63); the launches traced: 161 us -> 102 us
  Pallas kernels: 144 us -> 101 us
  local copies, waits for them, and re-layouts: 10.4 us -> 0 us
  between operations: 3.37 us -> 0.64 us
  other arithmetic: 2.71 us -> 0 us
    pallas_call x1, Pallas kernels: 144 us -> 97.4 us  [body(): pl.pallas_call(kernel, out_shape=[jax.ShapeDtypeStruct(thickness.shape, f...]
    unnamed x4 -> x0, local copies, waits for them, and re-layouts: 6.53 us -> none
    pallas_call x0 -> x1, Pallas kernels: none -> 3.7 us  [body(): pl.pallas_call(copy_kernel, out_shape=[jax.ShapeDtypeStruct(thickness.sha...]
where the time goes in v2:
time: 102 us
  Pallas kernels  101 us (99%)
    pallas_call x1, Pallas kernels, body(): pl.pallas_call(kernel, out_shape=[jax.ShapeDtypeStruct(thickness.shape, f...  97.4 us
    pallas_call x1, Pallas kernels, body(): pl.pallas_call(copy_kernel, out_shape=[jax.ShapeDtypeStruct(thickness.sha...  3.7 us

profile of v2, /device:TPU:1, one launch (start us, length us, event | category | flops | bytes accessed | tf_op | source)
XLA Modules:
  0.0 101.8 jit_solution(9352287007329044585)
XLA Ops:
  0.6 97.4 %shard_map.130 = (f32[8,48,384]{2,1,0:T(8,128)}, f32[8,48,384]{2,1,0:T(8,128)}, f32[8,48,384]{2,1,0:T(8,128)}) custom-call(s32[2,144]{1,0:T(2,128)} %bitcast.8, s32[4,108]{1,0:T(4,128)} %bitcast.9, s32[2,4]{1,0:T(2,128)} %rotation.1, bf16[24,144,256]{2,1,0:T(8,128)(2,1)} %bitcast.7, bf16[144,256,256]{2,1,0:T(8,128)(2,1)} %bitcast.6, f32[4,48,384]{2,1,0:T(8,128)} %basis.1, ...), custom_call_target="tpu_custom_call" | custom-call | tf_op jit(solution)/shard_map/pallas_call | solution.py:618
  98.1 3.7 %shard_map.131 = (f32[8,48,384]{2,1,0:T(8,128)}, f32[8,48,384]{2,1,0:T(8,128)}, f32[8,48,384]{2,1,0:T(8,128)}) custom-call(f32[8,48,384]{2,1,0:T(8,128)} %get-tuple-element.6.depth, f32[8,48,384]{2,1,0:T(8,128)} %get-tuple-element.7.first, f32[8,48,384]{2,1,0:T(8,128)} %get-tuple-element.8.second), custom_call_target="tpu_custom_call" | custom-call | tf_op jit(solution)/shard_map/pallas_call | solution.py:635

commit v3 on v2

--- a/solution.py
+++ b/solution.py
@@ -11,8 +11,9 @@
 HALO = 4
 COURANT = 0.15
 HALF_GRADIENT = 0.15
+FACE_SCALE = 0.5 * COURANT
 LANES = 128
-GROUPS = 32
+GROUPS = 16
 NX = 4
 SEND_CHUNKS = 6
 LAG = 1
@@ -73,9 +74,6 @@
                     field.at[:, :, b * LANES : (b + 1) * LANES], state_in.at[i, b], field_sem.at[3 + i * blocks + b]
                 )
             )
-    for copy in field_copies:
-        copy.start()
-
     owners = flows + 1
     square = (LANES, LANES)
     row_id = lax.broadcasted_iota(jnp.int32, square, 0)
@@ -170,6 +168,8 @@
         return carry
 
     lax.fori_loop(0, w_chunks, term_chunk, 0)
+    for copy in field_copies:
+        copy.start()
 
     table_copy.wait()
     pl.semaphore_wait(barrier, len(partners))
@@ -298,8 +298,8 @@
             for b in range(blocks):
                 block = grid_raw[k, at, b * LANES : (b + 1) * LANES]
                 for j in picks:
-                    metric[k, base + j, b] = spread(block, j)
-            side = jnp.where(lane < LANES // 2, grid_side[0, k, at, :] * keep_right, grid_side[1, k, at, :] * keep_left)
+                    metric[k, base + j, b] = spread(block, j) * FACE_SCALE
+            side = jnp.where(lane < LANES // 2, grid_side[0, k, at, :] * (keep_right * FACE_SCALE), grid_side[1, k, at, :] * (keep_left * FACE_SCALE))
             for j in picks:
                 metric[k, base + j, blocks] = spread(side, j)
         return carry
@@ -337,8 +337,8 @@
             xa[2, r + EDGE, b] = start(2) + bases[2, r, b] * east + bases[3, r, b] * north
         return carry
 
-    lax.fori_loop(0, HALO, regrid, 0)
-    lax.fori_loop(rows - HALO, rows, regrid, 0)
+    lax.fori_loop(0, HALO, regrid, 0, unroll=4)
+    lax.fori_loop(rows - HALO, rows, regrid, 0, unroll=4)
 
     def halo_copy(i, src, dst, to):
         return pltpu.make_async_remote_copy(
@@ -352,51 +352,43 @@
     for copy in row_copies:
         copy.start()
 
-    lax.fori_loop(HALO, rows - HALO, regrid, 0)
-
-    group = lane // HALO
-    packs = packed.shape[1]
-    for side in range(2):
-        for v in range(packs):
-            total = jnp.zeros(shape, jnp.float32)
-            for g in range(GROUPS):
-                item = v * GROUPS + g
-                if item >= 3 * rows:
-                    break
-                edge = xa[item % 3, item // 3 + EDGE, 0 if side == 0 else blocks - 1]
-                shift = (HALO * g + (HALO if side else 0)) % LANES
-                moved = pltpu.roll(edge, shift, 1) if shift else edge
-                total = jnp.where(group == g, moved, total)
-            packed[side, v] = total
+    lax.fori_loop(HALO, rows - HALO, regrid, 0, unroll=4)
+
+    group = lax.rem(lane + HALO, LANES) // (2 * HALO)
+    packs = packed.shape[0]
+    for v in range(packs):
+        total = jnp.zeros(shape, jnp.float32)
+        for g in range(GROUPS):
+            item = v * GROUPS + g
+            f, i = item % 3, item // 3 + EDGE
+            edges = jnp.where(lane < LANES // 2, xa[f, i, 0], xa[f, i, blocks - 1])
+            moved = pltpu.roll(edges, 2 * HALO * g, 1) if g else edges
+            total = jnp.where(group == g, moved, total)
+        packed[v] = total
 
     strip_copies = []
     for side, dx in ((0, -1), (1, 1)):
         strip_copies += [
-            halo_copy(2 + 3 * side, packed.at[side], strips.at[side, 0:packs], (dx, 0)),
-            halo_copy(3 + 3 * side, packed.at[side, 0:1], strips.at[side, packs + 1 : packs + 2], (dx, -1)),
-            halo_copy(4 + 3 * side, packed.at[side, packs - 1 : packs], strips.at[side, packs : packs + 1], (dx, 1)),
+            halo_copy(2 + 3 * side, packed, strips.at[side, 0:packs], (dx, 0)),
+            halo_copy(3 + 3 * side, packed.at[0:1], strips.at[side, packs + 1 : packs + 2], (dx, -1)),
+            halo_copy(4 + 3 * side, packed.at[packs - 1 : packs], strips.at[side, packs : packs + 1], (dx, 1)),
         ]
     for copy in strip_copies:
         copy.start()
     for copy in strip_copies:
         copy.wait_recv()
 
+    low_half = lax.rem(lane // HALO, 2) == 0
+    halos = [
+        jnp.where(low_half, strips[0, v] * keep_right, strips[1, v] * keep_left) for v in range(packs + 2)
+    ]
     for r in range(-HALO, rows + HALO):
         for f in range(3):
             item = 3 * (r % rows) + f
             g = item % GROUPS
-            v = item // GROUPS
-            if r < 0:
-                v = packs
-            elif r >= rows:
-                v = packs + 1
-            from_right = pltpu.roll(strips[0, v], (LANES - HALO * g) % LANES, 1) if g else strips[0, v]
-            from_left = pltpu.roll(strips[1, v], (LANES - HALO - HALO * g) % LANES, 1) if g < GROUPS - 1 else strips[1, v]
-            xa[f, r + EDGE, blocks] = jnp.where(
-                lane < HALO,
-                from_right * keep_right,
-                jnp.where(lane >= LANES - HALO, from_left * keep_left, 0.0),
-            )
+            v = packs if r < 0 else packs + 1 if r >= rows else item // GROUPS
+            xa[f, r + EDGE, blocks] = pltpu.roll(halos[v], LANES - 2 * HALO * g, 1) if g else halos[v]
+
     ring = blocks + 1
     is_first = lane == 0
     is_last = lane == LANES - 1
@@ -423,11 +415,13 @@
             con_second.append(metric[2, i, b] * first + metric[1, i, b] * second)
         return depth, con_first, con_second
 
+    def upwind(face, depth_low, depth_high):
+        return face * jnp.where(face > 0.0, depth_low, depth_high)
+
     def row_flux(second_low, second_high, depth_low, depth_high):
         out = []
         for b in range(ring):
-            face = 0.5 * (second_low[b] + second_high[b])
-            out.append(jnp.maximum(face, 0.0) * depth_low[b] + jnp.minimum(face, 0.0) * depth_high[b])
+            out.append(upwind(second_low[b] + second_high[b], depth_low[b], depth_high[b]))
         return out
 
     tiles = n_ty // PANELS
@@ -482,19 +476,19 @@
             depth_right, first_right = from_next(depth), from_next(con_first)
             depth_left, first_left = from_before(depth), from_before(con_first)
             for b in range(ring):
-                face = 0.5 * (con_first[b] + first_right[b])
+                face = con_first[b] + first_right[b]
                 if b == blocks - 1:
                     face = face * wall_right
                 if b == blocks:
                     face = face * wall_left
-                flux_right = jnp.maximum(face, 0.0) * depth[b] + jnp.minimum(face, 0.0) * depth_right[b]
-                face = 0.5 * (con_first[b] + first_left[b])
+                flux_right = upwind(face, depth[b], depth_right[b])
+                face = con_first[b] + first_left[b]
                 if b == blocks:
                     face = face * wall_right_halo
                 if b == 0:
                     face = face * wall_left_tile
-                flux_left = jnp.maximum(face, 0.0) * depth_left[b] + jnp.minimum(face, 0.0) * depth[b]
-                new_depth = depth[b] - COURANT * ((flux_right - flux_left) + (flux_above[b] - flux_below[b]))
+                flux_left = upwind(face, depth_left[b], depth[b])
+                new_depth = depth[b] - ((flux_right - flux_left) + (flux_above[b] - flux_below[b]))
                 new_first = src[1, i + j, b] - HALF_GRADIENT * (depth_right[b] - depth_left[b])
                 new_second = src[2, i + j, b] - HALF_GRADIENT * (depth_after[b] - depth_before[b])
                 store(i + j, b, (new_depth, new_first, new_second))
@@ -531,15 +525,22 @@
         elif step < STEPS - 1:
             sweep(0, groups + 2)
         else:
-            sweep(1, groups + 1)
-
-    out_copies = [
-        pltpu.make_async_copy(out_v.at[f, b], out.at[:, :, b * LANES : (b + 1) * LANES], out_sem.at[f, b])
-        for f, out in enumerate((out_depth, out_first, out_second))
-        for b in range(blocks)
-    ]
-    for copy in out_copies:
-        copy.start()
+            out_copies = []
+            half = rows // 2
+            for part in range(2):
+                sweep(1 + part * groups // 2, 1 + (part + 1) * groups // 2)
+                span = slice(part * half, (part + 1) * half)
+                copies = [
+                    pltpu.make_async_copy(
+                        out_v.at[f, b, :, span], out.at[:, span, b * LANES : (b + 1) * LANES], out_sem.at[part, f, b]
+                    )
+                    for f, out in enumerate((out_depth, out_first, out_second))
+                    for b in range(blocks)
+                ]
+                for copy in copies:
+                    copy.start()
+                out_copies += copies
+
     for d in range(1, flows + 1):
 
         def sent(c, carry):
@@ -593,7 +594,7 @@
         vmem((3, rows + 16, cols), f32),
         vmem((2, 3, rows + 16, LANES), f32),
         vmem((4, rows, cols), f32),
-        vmem((2, packs, levels, LANES), f32),
+        vmem((packs, levels, LANES), f32),
         vmem((2, packs + 2, levels, LANES), f32),
         vmem((8, 2 * LANES), jnp.int32),
         vmem((8, LANES), jnp.int32),
@@ -603,7 +604,7 @@
         dma,
         dma,
         dma((3 + 3 * blocks,)),
-        dma((3, blocks)),
+        dma((2, 3, blocks)),
         dma((flows, SEND_CHUNKS)),
         dma((flows, SEND_CHUNKS)),
         dma((flows, SEND_CHUNKS)),
@@ -630,22 +631,28 @@
         remap_weights.reshape(lat_rows, top * patch, cells),
         basis, inv_metric_diag, inv_metric_cross, thickness, wind_first, wind_second,
     )
-    spec = pl.BlockSpec((levels // 4, rows, cols), lambda i: (i, 0, 0))
     return tuple(
         pl.pallas_call(
             copy_kernel,
             out_shape=[jax.ShapeDtypeStruct(thickness.shape, f32)] * 3,
-            grid=(4,),
-            in_specs=[spec] * 3,
-            out_specs=[spec] * 3,
+            in_specs=[anywhere] * 3,
+            out_specs=[anywhere] * 3,
+            scratch_shapes=[vmem((3,) + thickness.shape, f32), dma((3,)), dma((3,))],
         )(*moved)
     )
 
 
-def copy_kernel(depth, first, second, out_depth, out_first, out_second):
-    out_depth[...] = depth[...]
-    out_first[...] = first[...]
-    out_second[...] = second[...]
+def copy_kernel(depth, first, second, out_depth, out_first, out_second, held, in_sem, out_sem):
+    pairs = ((depth, out_depth), (first, out_first), (second, out_second))
+    incoming = [pltpu.make_async_copy(src, held.at[i], in_sem.at[i]) for i, (src, _) in enumerate(pairs)]
+    outgoing = [pltpu.make_async_copy(held.at[i], dst, out_sem.at[i]) for i, (_, dst) in enumerate(pairs)]
+    for copy in incoming:
+        copy.start()
+    for arrived, copy in zip(incoming, outgoing):
+        arrived.wait()
+        copy.start()
+    for copy in outgoing:
+        copy.wait()
 
 
 def solution(mesh):

time: 102 us -> 99.5 us (0.975)
  Pallas kernels: 101 us -> 98.6 us
    pallas_call x1, Pallas kernels: 3.7 us -> 2.32 us  [body(): pl.pallas_call(copy_kernel, out_shape=[jax.ShapeDtypeStruct(thickness.sha...]
    pallas_call x1, Pallas kernels: 97.4 us -> 96.2 us  [body(): pl.pallas_call(kernel, out_shape=[jax.ShapeDtypeStruct(thickness.shape, f...]
where the time goes in v3:
time: 99.5 us; the launch traced here: 99.2 us
  Pallas kernels  98.6 us (99%)
    pallas_call x1, Pallas kernels, body(): pl.pallas_call(kernel, out_shape=[jax.ShapeDtypeStruct(thickness.shape, f...  96.2 us
    pallas_call x1, Pallas kernels, body(): pl.pallas_call(copy_kernel, out_shape=[jax.ShapeDtypeStruct(thickness.sha...  2.32 us

profile of v3, /device:TPU:1, one launch (start us, length us, event | category | flops | bytes accessed | tf_op | source)
XLA Modules:
  0.0 99.2 jit_solution(15496710399616807327)
XLA Ops:
  0.6 96.2 %shard_map.130 = (f32[8,48,384]{2,1,0:T(8,128)}, f32[8,48,384]{2,1,0:T(8,128)}, f32[8,48,384]{2,1,0:T(8,128)}) custom-call(s32[2,144]{1,0:T(2,128)} %bitcast.8, s32[4,108]{1,0:T(4,128)} %bitcast.9, s32[2,4]{1,0:T(2,128)} %rotation.1, bf16[24,144,256]{2,1,0:T(8,128)(2,1)} %bitcast.7, bf16[144,256,256]{2,1,0:T(8,128)(2,1)} %bitcast.6, f32[4,48,384]{2,1,0:T(8,128)} %basis.1, ...), custom_call_target="tpu_custom_call" | custom-call | tf_op jit(solution)/shard_map/pallas_call | solution.py:619
  96.9 2.3 %shard_map.131 = (f32[8,48,384]{2,1,0:T(8,128)}, f32[8,48,384]{2,1,0:T(8,128)}, f32[8,48,384]{2,1,0:T(8,128)}) custom-call(f32[8,48,384]{2,1,0:T(8,128)} %get-tuple-element.6.depth, f32[8,48,384]{2,1,0:T(8,128)} %get-tuple-element.7.first, f32[8,48,384]{2,1,0:T(8,128)} %get-tuple-element.8.second), custom_call_target="tpu_custom_call" | custom-call | tf_op jit(solution)/shard_map/pallas_call | solution.py:635

commit v4 on v3

--- a/solution.py
+++ b/solution.py
@@ -58,9 +58,11 @@
     def w_copy(chunk, slot):
         return pltpu.make_async_copy(wts.at[pl.ds(chunk * W_ROWS, W_ROWS)], wbuf.at[slot], w_sem.at[slot])
 
-    inc_copy = pltpu.make_async_copy(inc, inc_v, in_sem)
-    inc_copy.start()
+    def inc_copy(chunk, slot):
+        return pltpu.make_async_copy(inc.at[:, pl.ds(chunk * W_ROWS, W_ROWS)], inc_v.at[slot], in_sem.at[slot])
+
     for slot in range(W_SLOTS):
+        inc_copy(slot, slot).start()
         w_copy(slot, slot).start()
     field_copies = [
         pltpu.make_async_copy(diag, grid_raw.at[0:2, 8 : 8 + rows], field_sem.at[0]),
@@ -140,12 +142,11 @@
     term[entries] = zero_row
     acc[slots] = zero_row
 
-    inc_copy.wait()
-
     def term_chunk(chunk, carry):
         slot = lax.rem(chunk, W_SLOTS)
-        start = pl.multiple_of(chunk * W_ROWS, W_ROWS)
-        cells = inc_v[:, pl.ds(start, W_ROWS), :].astype(jnp.float32)
+        start = chunk * W_ROWS
+        inc_copy(chunk, slot).wait()
+        cells = inc_v[slot].astype(jnp.float32)
         pairs = cells.shape[0]
         half0[...] = cells[:, :, :LANES].reshape(pairs * W_ROWS, LANES)
         half1[...] = cells[:, :, LANES:].reshape(pairs * W_ROWS, LANES)
@@ -163,6 +164,7 @@
 
         @pl.when(chunk + W_SLOTS < w_chunks)
         def _():
+            inc_copy(chunk + W_SLOTS, slot).start()
             w_copy(chunk + W_SLOTS, slot).start()
 
         return carry
@@ -511,7 +513,8 @@
 
         def sweep(first, end, src=src, store=store):
             lax.fori_loop(
-                first, end, lambda g, flux: tuple(advance_group(src, store, g, flux)), tuple(flux_into(src, first))
+                first, end, lambda g, flux: tuple(advance_group(src, store, g, flux)), tuple(flux_into(src, first)),
+                unroll=2,
             )
 
         if step == 0:
@@ -577,7 +580,7 @@
     vmem, dma = pltpu.VMEM, pltpu.SemaphoreType.DMA
     scratch = [
         vmem((W_SLOTS, W_ROWS, top * patch, cells), jnp.bfloat16),
-        vmem((pairs, lat_rows, cells), jnp.bfloat16),
+        vmem((W_SLOTS, pairs, W_ROWS, cells), jnp.bfloat16),
         vmem((pairs * W_ROWS, LANES), f32),
         vmem((pairs * W_ROWS, LANES), f32),
         vmem((entries + 1, pairs, LANES), f32),
@@ -601,7 +604,7 @@
         vmem((16, LANES), jnp.int32),
         pltpu.SMEM((16, LANES), jnp.int32),
         dma((W_SLOTS,)),
-        dma,
+        dma((W_SLOTS,)),
         dma,
         dma((3 + 3 * blocks,)),
         dma((2, 3, blocks)),

time: 99.5 us -> 95.7 us (0.962)
  Pallas kernels: 98.6 us -> 94.8 us
    pallas_call x1, Pallas kernels: 96.2 us -> 92.5 us  [body(): pl.pallas_call(kernel, out_shape=[jax.ShapeDtypeStruct(thickness.shape, f...]
where the time goes in v4:
time: 95.7 us; the launch traced here: 95.5 us
  Pallas kernels  94.8 us (99%)
    pallas_call x1, Pallas kernels, body(): pl.pallas_call(kernel, out_shape=[jax.ShapeDtypeStruct(thickness.shape, f...  92.5 us
    pallas_call x1, Pallas kernels, body(): pl.pallas_call(copy_kernel, out_shape=[jax.ShapeDtypeStruct(thickness.sha...  2.32 us

profile of v4, /device:TPU:1, one launch (start us, length us, event | category | flops | bytes accessed | tf_op | source)
XLA Modules:
  0.0 95.5 jit_solution(16196509011413664492)
XLA Ops:
  0.6 92.5 %shard_map.130 = (f32[8,48,384]{2,1,0:T(8,128)}, f32[8,48,384]{2,1,0:T(8,128)}, f32[8,48,384]{2,1,0:T(8,128)}) custom-call(s32[2,144]{1,0:T(2,128)} %bitcast.8, s32[4,108]{1,0:T(4,128)} %bitcast.9, s32[2,4]{1,0:T(2,128)} %rotation.1, bf16[24,144,256]{2,1,0:T(8,128)(2,1)} %bitcast.7, bf16[144,256,256]{2,1,0:T(8,128)(2,1)} %bitcast.6, f32[4,48,384]{2,1,0:T(8,128)} %basis.1, ...), custom_call_target="tpu_custom_call" | custom-call | tf_op jit(solution)/shard_map/pallas_call | solution.py:622
  93.2 2.3 %shard_map.131 = (f32[8,48,384]{2,1,0:T(8,128)}, f32[8,48,384]{2,1,0:T(8,128)}, f32[8,48,384]{2,1,0:T(8,128)}) custom-call(f32[8,48,384]{2,1,0:T(8,128)} %get-tuple-element.6.depth, f32[8,48,384]{2,1,0:T(8,128)} %get-tuple-element.7.first, f32[8,48,384]{2,1,0:T(8,128)} %get-tuple-element.8.second), custom_call_target="tpu_custom_call" | custom-call | tf_op jit(solution)/shard_map/pallas_call | solution.py:638

commit v5 on v4

--- a/solution.py
+++ b/solution.py
@@ -319,7 +319,7 @@
                 acc[base + i] = recv[d - 1, c * per + i] + acc[table[owners + d, c * per + i]]
                 return inner
 
-            lax.fori_loop(0, per, add, 0, unroll=6)
+            lax.fori_loop(0, per, add, 0, unroll=per)
         return carry
 
     lax.fori_loop(0, SEND_CHUNKS, receive_chunk, 0)
@@ -514,7 +514,7 @@
         def sweep(first, end, src=src, store=store):
             lax.fori_loop(
                 first, end, lambda g, flux: tuple(advance_group(src, store, g, flux)), tuple(flux_into(src, first)),
-                unroll=2,
+                unroll=max(2, (end - first) // 2),
             )
 
         if step == 0:

time: 95.7 us -> 95 us (level)
  no operation moved by 1% of the time
where the time goes in v5:
time: 95 us; the launch traced here: 94.7 us
  Pallas kernels  94.1 us (99%)
    pallas_call x1, Pallas kernels, body(): pl.pallas_call(kernel, out_shape=[jax.ShapeDtypeStruct(thickness.shape, f...  91.8 us
    pallas_call x1, Pallas kernels, body(): pl.pallas_call(copy_kernel, out_shape=[jax.ShapeDtypeStruct(thickness.sha...  2.32 us

profile of v5, /device:TPU:1, one launch (start us, length us, event | category | flops | bytes accessed | tf_op | source)
XLA Modules:
  0.0 94.7 jit_solution(12874752094657240035)
XLA Ops:
  0.6 91.8 %shard_map.130 = (f32[8,48,384]{2,1,0:T(8,128)}, f32[8,48,384]{2,1,0:T(8,128)}, f32[8,48,384]{2,1,0:T(8,128)}) custom-call(s32[2,144]{1,0:T(2,128)} %bitcast.8, s32[4,108]{1,0:T(4,128)} %bitcast.9, s32[2,4]{1,0:T(2,128)} %rotation.1, bf16[24,144,256]{2,1,0:T(8,128)(2,1)} %bitcast.7, bf16[144,256,256]{2,1,0:T(8,128)(2,1)} %bitcast.6, f32[4,48,384]{2,1,0:T(8,128)} %basis.1, ...), custom_call_target="tpu_custom_call" | custom-call | tf_op jit(solution)/shard_map/pallas_call | solution.py:622
  92.4 2.3 %shard_map.131 = (f32[8,48,384]{2,1,0:T(8,128)}, f32[8,48,384]{2,1,0:T(8,128)}, f32[8,48,384]{2,1,0:T(8,128)}) custom-call(f32[8,48,384]{2,1,0:T(8,128)} %get-tuple-element.6.depth, f32[8,48,384]{2,1,0:T(8,128)} %get-tuple-element.7.first, f32[8,48,384]{2,1,0:T(8,128)} %get-tuple-element.8.second), custom_call_target="tpu_custom_call" | custom-call | tf_op jit(solution)/shard_map/pallas_call | solution.py:638
